TPU v7x, 32 devices: a whole 2x2x4 slice. The times are simulated.
32 devices in a mesh: dp: 4 (over x, core), seq: 8 (over z, y).
Axes of the slice: x: 2, y: 2, z: 4, core: 2. Of those that a mesh axis runs over, the one named last changes fastest.
Arguments:
- xbc_in: bfloat16 [4, 2048, 2816], P('dp', 'seq'), may hold values from -4 to 4
- conv_weight: float32 [4, 2816], replicated, may hold values from -3 to 3
- conv_bias: float32 [2816], replicated, may hold values from -3 to 3
- step_sizes: float32 [4, 40, 2048], P('dp', None, 'seq'), may hold values from 0 to 1, as said below
- decay_rates: float32 [40], replicated, may hold values from 0.7 to 1.4
- skip_gain: float32 [40], replicated, may hold values from 0.5 to 1.5
- grad_out: bfloat16 [4, 2048, 2560], P('dp', 'seq'), may hold values from -0.75 to 0.75
Outputs:
- grad_xbc: bfloat16 [4, 2048, 2816], P('dp', 'seq')
- grad_steps: float32 [4, 40, 2048], P('dp', None, 'seq')
- grad_conv_weight: float32 [4, 2816], replicated
- grad_conv_bias: float32 [2816], replicated
- grad_rates: float32 [40], replicated
- grad_skip: float32 [40], replicated
Inputs may be any that keep to these rules, and one draw needn't show every extreme that they name: `step_sizes`: positive step sizes.
All inputs are finite; a program needn't handle non-finite values.
Results may differ from a plain program's by a relative error of at most 0.0056.
Values may be sent and summed in bfloat16 or wider, within the bound.
A program may use at most 192 MiB of HBM per device.

v0:
```python
import jax
import jax.numpy as jnp
from jax import lax
from jax.sharding import PartitionSpec as P

HEADS = 40
HEAD_DIM = 64
STATE = 128
GROUP = 256
KCONV = 4


def shifted(array, axis, by):
    length = lax.axis_size(axis)
    pairs = [(i, i + by) for i in range(length) if 0 <= i + by < length]
    return lax.ppermute(array, axis, pairs)


def carried_in(array, axis, combine, identity, reverse):
    length, place = (lax.axis_size(axis), lax.axis_index(axis))
    everything = jax.tree.map(lambda part: lax.all_gather(part, axis), array)
    start = jax.tree.map(
        lambda part, zero: jnp.broadcast_to(jnp.asarray(zero, part.dtype), part.shape),
        array,
        identity,
    )

    def lap(k, before):
        at = length - 1 - k if reverse else k
        reached = at > place if reverse else at < place
        new = combine(before, jax.tree.map(lambda part: part[at], everything))
        return jax.tree.map(lambda a, b: jnp.where(reached, a, b), new, before)

    return lax.fori_loop(0, length, lap, start)


def silu_pair(pre_act):
    sigmoid_v = jax.nn.sigmoid(pre_act)
    return (pre_act * sigmoid_v, sigmoid_v * (1.0 + pre_act * (1.0 - sigmoid_v)))


def block_locals(z_block, dy_block, cum_log):
    x_width = HEADS * HEAD_DIM
    b_proj = z_block[:, x_width : x_width + STATE]
    c_proj = z_block[:, x_width + STATE :]
    log_end = cum_log[:, -1:]
    tail_wide = jnp.repeat(jnp.exp(log_end - cum_log).T, HEAD_DIM, axis=1)
    head_wide = jnp.repeat(jnp.exp(cum_log).T, HEAD_DIM, axis=1)
    x_weighted = (z_block[:, :x_width].astype(jnp.float32) * tail_wide).astype(jnp.bfloat16)
    dy_weighted = (dy_block.astype(jnp.float32) * head_wide).astype(jnp.bfloat16)
    contract_rows = (((0,), (0,)), ((), ()))
    s_local = lax.dot_general(x_weighted, b_proj, contract_rows, preferred_element_type=jnp.float32)
    u_local = lax.dot_general(
        dy_weighted, c_proj, contract_rows, preferred_element_type=jnp.float32
    )
    s_local = s_local.reshape(HEADS, HEAD_DIM, STATE)
    u_local = u_local.reshape(HEADS, HEAD_DIM, STATE)
    return (s_local, u_local, x_weighted, dy_weighted)


def block_grads(
    z_block, dy_block, cum_log, x_weighted, dy_weighted, start_state, end_adjoint, skip_gain
):
    x_width = HEADS * HEAD_DIM
    x_flat = z_block[:, :x_width]
    b_proj = z_block[:, x_width : x_width + STATE]
    c_proj = z_block[:, x_width + STATE :]
    log_end = cum_log[:, -1:]
    contract_last = (((1,), (1,)), ((), ()))
    gram_bc = lax.dot_general(b_proj, c_proj, contract_last, preferred_element_type=jnp.float32)
    row_index = lax.broadcasted_iota(jnp.int32, (GROUP, GROUP), 0)
    col_index = lax.broadcasted_iota(jnp.int32, (GROUP, GROUP), 1)
    causal = (row_index >= col_index)[None]
    upper = (row_index <= col_index)[None]
    log_gap = cum_log[:, :, None] - cum_log[:, None, :]
    decay_lower = jnp.where(causal, jnp.exp(jnp.where(causal, log_gap, 0.0)), 0.0)
    rise_gap = cum_log[:, None, :] - cum_log[:, :, None]
    decay_upper = jnp.where(upper, jnp.exp(jnp.where(upper, rise_gap, 0.0)), 0.0)
    x_heads = x_flat.reshape(GROUP, HEADS, HEAD_DIM)
    dy_heads = dy_block.reshape(GROUP, HEADS, HEAD_DIM)
    inner_dx = jnp.einsum("thp,shp->hts", dy_heads, x_heads, preferred_element_type=jnp.float32)
    weights = decay_lower * inner_dx
    k_matrix = (decay_upper * gram_bc[None]).astype(jnp.bfloat16)
    m_terms = weights * gram_bc.T[None]
    w_summed = jnp.sum(weights, axis=0).astype(jnp.bfloat16)
    states_low = start_state.astype(jnp.bfloat16).reshape(x_width, STATE)
    adjoint_low = end_adjoint.astype(jnp.bfloat16).reshape(x_width, STATE)
    b_adjoint = lax.dot_general(
        b_proj, adjoint_low, contract_last, preferred_element_type=jnp.float32
    )
    tail_wide = jnp.repeat(jnp.exp(log_end - cum_log).T, HEAD_DIM, axis=1)
    intra_dx = jnp.einsum("hts,shp->thp", k_matrix, dy_heads, preferred_element_type=jnp.float32)
    dx_state = intra_dx.reshape(GROUP, x_width) + tail_wide * b_adjoint
    contract_rows = (((0,), (0,)), ((), ()))
    grad_bproj = lax.dot_general(
        w_summed, c_proj, contract_rows, preferred_element_type=jnp.float32
    )
    grad_bproj = grad_bproj + jnp.dot(x_weighted, adjoint_low, preferred_element_type=jnp.float32)
    grad_cproj = jnp.dot(w_summed, b_proj, preferred_element_type=jnp.float32)
    grad_cproj = grad_cproj + jnp.dot(dy_weighted, states_low, preferred_element_type=jnp.float32)
    c_state = lax.dot_general(c_proj, states_low, contract_last, preferred_element_type=jnp.float32)
    x_float = x_flat.astype(jnp.float32)
    dy_float = dy_block.astype(jnp.float32)
    q_terms = jnp.sum((c_state * dy_float).reshape(GROUP, HEADS, HEAD_DIM), axis=2).T
    r_terms = jnp.sum((b_adjoint * x_float).reshape(GROUP, HEADS, HEAD_DIM), axis=2).T
    col_sums = jnp.sum(m_terms, axis=1)
    row_sums = jnp.sum(m_terms, axis=2)
    term_one = jnp.cumsum(col_sums - row_sums, axis=1) + row_sums
    term_two = jnp.flip(jnp.cumsum(jnp.flip(jnp.exp(cum_log) * q_terms, 1), axis=1), 1)
    term_three = jnp.cumsum(jnp.exp(log_end - cum_log) * r_terms, axis=1)
    term_four = jnp.exp(log_end) * jnp.sum(end_adjoint * start_state, axis=(1, 2))[:, None]
    own_terms = jnp.sum((x_float * dx_state).reshape(GROUP, HEADS, HEAD_DIM), axis=2).T
    grad_log = term_one + term_two + term_three + term_four - own_terms
    dx_full = dx_state + jnp.repeat(skip_gain, HEAD_DIM)[None, :] * dy_float
    grad_z = jnp.concatenate([dx_full, grad_bproj, grad_cproj], axis=1)
    return (grad_z, grad_log)


def compose(earlier, later):
    return (earlier[0] * later[0], later[0][:, :, None, None] * earlier[1] + later[1])


def shards(xbc_in, conv_weight, conv_bias, step_sizes, decay_rates, skip_gain, grad_out):
    seq_count, tokens, channels = xbc_in.shape
    rim_len = KCONV - 1
    x_width = HEADS * HEAD_DIM
    block_count = tokens // GROUP
    before = shifted(xbc_in[:, tokens - rim_len :, :], "seq", 1)
    padded_in = jnp.concatenate([before, xbc_in], axis=1)
    pre_act = jnp.zeros((seq_count, tokens, channels), jnp.float32) + conv_bias[None, None, :]
    for tap_index in range(KCONV):
        pre_act = pre_act + conv_weight[tap_index][None, None, :] * padded_in[
            :, tap_index : tap_index + tokens
        ].astype(jnp.float32)
    activated, derivative = silu_pair(pre_act)
    z_seq = activated.astype(jnp.bfloat16)
    skip_terms = (z_seq[:, :, :x_width].astype(jnp.float32) * grad_out.astype(jnp.float32)).reshape(
        seq_count, tokens, HEADS, HEAD_DIM
    )
    local_skip = jnp.sum(skip_terms, axis=(0, 1, 3))
    log_steps = -(step_sizes * decay_rates[None, :, None])
    cum_log = jnp.cumsum(log_steps.reshape(seq_count, HEADS, block_count, GROUP), axis=3)
    locals_fn = jax.vmap(block_locals)
    grads_fn = jax.vmap(block_grads, in_axes=(0, 0, 0, 0, 0, 0, 0, None))
    block_index = 0
    z_parts = [z_seq]
    dy_parts = [grad_out]
    log_parts = [cum_log[:, :, block_index]]
    local_items = [locals_fn(z_parts[block_index], dy_parts[block_index], log_parts[block_index])]
    decay_ends = [jnp.exp(log_parts[block_index][:, :, -1])]
    dev_decay = jnp.ones((seq_count, HEADS), jnp.float32)
    dev_state = jnp.zeros((seq_count, HEADS, HEAD_DIM, STATE), jnp.float32)
    dev_adjoint = jnp.zeros((seq_count, HEADS, HEAD_DIM, STATE), jnp.float32)
    block_index = 0
    dev_state = decay_ends[block_index][:, :, None, None] * dev_state + local_items[block_index][0]
    dev_decay = dev_decay * decay_ends[block_index]
    for block_index in reversed(range(block_count)):
        dev_adjoint = (
            decay_ends[block_index][:, :, None, None] * dev_adjoint + local_items[block_index][1]
        )
    identity_pair = (jnp.ones_like(dev_decay), jnp.zeros_like(dev_state))
    enter_pair = carried_in((dev_decay, dev_state), "seq", compose, identity_pair, False)
    leave_pair = carried_in((dev_decay, dev_adjoint), "seq", compose, identity_pair, True)
    entering = enter_pair[1]
    leaving = leave_pair[1]
    block_index = 0
    block_starts = [entering]
    adjoint_run = leaving
    block_ends = [adjoint_run] * block_count
    for block_index in reversed(range(block_count)):
        block_ends[block_index] = adjoint_run
        adjoint_run = (
            decay_ends[block_index][:, :, None, None] * adjoint_run + local_items[block_index][1]
        )
    block_index = 0
    grad_piece, log_piece = grads_fn(
        z_parts[block_index],
        dy_parts[block_index],
        log_parts[block_index],
        local_items[block_index][2],
        local_items[block_index][3],
        block_starts[block_index],
        block_ends[block_index],
        skip_gain,
    )
    grad_pre = grad_piece * derivative
    tail_zeros = jnp.zeros((seq_count, rim_len, channels), jnp.float32)
    padded_grad = jnp.concatenate([grad_pre, tail_zeros], axis=1)
    front_rows = jnp.concatenate([tail_zeros, grad_pre[:, :rim_len]], axis=1)
    grad_in = jnp.zeros((seq_count, tokens, channels), jnp.float32)
    partial_rows = jnp.zeros((seq_count, rim_len, channels), jnp.float32)
    for tap_index in range(KCONV):
        tap_start = rim_len - tap_index
        grad_in = (
            grad_in
            + conv_weight[tap_index][None, None, :] * padded_grad[:, tap_start : tap_start + tokens]
        )
        partial_rows = (
            partial_rows
            + conv_weight[tap_index][None, None, :] * front_rows[:, tap_start : tap_start + rim_len]
        )
    incoming = shifted(partial_rows, "seq", -1)
    grad_in = jnp.concatenate(
        [grad_in[:, : tokens - rim_len], grad_in[:, tokens - rim_len :] + incoming], axis=1
    )
    grad_taps = []
    for tap_index in range(KCONV):
        grad_taps.append(
            jnp.sum(
                grad_pre * padded_in[:, tap_index : tap_index + tokens].astype(jnp.float32),
                axis=(0, 1),
            )
        )
    local_weight = jnp.stack(grad_taps)
    local_bias = jnp.sum(grad_pre, axis=(0, 1))
    local_rates = -jnp.sum(step_sizes * log_piece, axis=(0, 2))
    grad_steps = -decay_rates[None, :, None] * log_piece
    grad_weight, grad_bias, grad_rates, grad_skip = lax.psum(
        (local_weight, local_bias, local_rates, local_skip), ("dp", "seq")
    )
    return (grad_in.astype(jnp.bfloat16), grad_steps, grad_weight, grad_bias, grad_rates, grad_skip)


def solution(mesh):
    return jax.shard_map(
        shards,
        mesh=mesh,
        in_specs=(
            P("dp", "seq", None),
            P(),
            P(),
            P("dp", None, "seq"),
            P(),
            P(),
            P("dp", "seq", None),
        ),
        out_specs=(P("dp", "seq", None), P("dp", None, "seq"), P(), P(), P(), P()),
        check_vma=False,
    )
```

profile of v0, /device:TPU:0, one launch (start us, length us, event | category | flops | bytes accessed | tf_op | source)
XLA Modules:
  0.0 455.2 jit_solution(9442393035926646633)
XLA Ops:
  8.0 4.9 %collective-permute-start = (bf16[1,3,2816]{2,1,0:T(4,128)(2,1)S(1)}, bf16[1,3,2816]{2,1,0:T(4,128)(2,1)S(1)}, u32[]{:S(2)}, u32[]{:S(2)}) collective-permute-start(bf16[1,3,2816]{2,1,0:T(4,128)(2,1)S(1)} %slice.105), channel_id=1, source_target_pairs={{0,1},{1,2},{2,3},{3,4},{4,5},{5,6},{6,7},{8,9},{9,10},{10,11},{11... | collective-permute-start | bytes 50696 | tf_op jit(solution)/shard_map/ppermute | solution.py:16
  16.6 3.3 copy.237
  20.0 2.0 fusion.62
  24.2 4.4 multiply_convert_fusion.2
  36.1 3.2 copy.244
  39.3 3.6 copy.241
  42.9 19.1 %all-gather = f32[8,40,1]{1,2,0:T(1,128)S(1)} all-gather(f32[1,40,1]{1,2,0:T(1,128)S(1)} %get-tuple-element.428), channel_id=2, replica_groups=mesh['dp'=4,'seq'=8] {'seq'}, dimensions={0}, use_global_device_ids=true | all-gather | bytes 1440 | tf_op jit(solution)/shard_map/all_gather | solution.py:21
  63.3 5.4 %fusion.2 = f32[40,256,64]{1,2,0:T(8,128)} fusion(bf16[256,40,64]{0,2,1:T(8,128)(2,1)} %bitcast.195, f32[256,256]{0,1:T(8,128)S(1)} %copy.230, f32[40,256]{1,0:T(8,128)S(1)} %bitcast_add_fusion.3, pred[256,256]{0,1:T(8,128)(4,1)S(1)} %iota_compare_fusion.1), kind=kOutput, calls=%fused_computation.10 | convolution fusion | flops 348651520 | bytes 4300800 | tf_op jit(solution)/shard_map/vmap(hts,shp->thp)/dot_general | solution.py:92
  68.7 3.3 copy.242
  72.0 110.4 %all-gather.6.cloned.1.call-done = f32[320,64,128]{2,1,0:T(8,128)} async-done(((f32[40,64,128]{2,1,0:T(8,128)}), f32[320,64,128]{2,1,0:T(8,128)}) %all-gather.6.cloned.1.call-update) | async-done | bytes 10485776 | tf_op jit(solution)/shard_map/all_gather | solution.py:21
  182.3 13.3 %while.30 = (s32[]{:T(128)}, f32[1,40,64,128]{3,2,1,0:T(8,128)S(1)}, s32[]{:T(128)}, f32[8,1,40]{2,1,0:T(1,128)S(1)}, f32[8,1,40,64,128]{4,3,2,1,0:T(8,128)}, /*index=5*/s32[]{:T(128)}, s32[]{:T(128)}, s32[]{:T(128)}, s32[]{:T(128)}) while((s32[]{:T(128)}, f32[1,40,64,128]{3,2,1,0:T(8,128)S(1)}, s32[]{:T(128)}, ...), condition=%wide.region_3.4_spmd.clone, body=%wide.region_2.3_spmd.clone.sunk | while | flops 1310728 | bytes 3932815 | solution.py:34
  195.8 8.9 %convert_multiply_fusion.1 = (f32[1,256,2560]{2,1,0:T(8,128)}, f32[1,256,2560]{2,1,0:T(8,128)}, f32[1,256,2560]{2,1,0:T(8,128)}, f32[2560]{0:T(1024)}, bf16[2560,256]{0,1:T(8,128)(2,1)}) fusion(f32[256,2560]{1,0:T(8,128)} %copy.242, f32[256,2560]{1,0:T(8,128)} %copy.241, bf16[1,256,2816]{2,1,0:T(8,128)(2,1)} %copy-done.2, ...), kind=kOutput, calls=%fused_computation.17 | convolution fusion | flops 175633920 | bytes 20402176 | tf_op jit(solution)/shard_map/vmap()/dot_general | solution.py:88
  206.4 2.4 convolution_add_fusion
  210.0 2.5 slice.138
  212.4 2.5 copy.243
  214.9 7.5 %multiply_reduce_fusion.1 = (f32[40,256]{1,0:T(8,128)S(1)}, f32[40,256]{1,0:T(8,128)S(1)}, bf16[256,256]{0,1:T(8,128)(2,1)S(1)}) fusion(f32[256,256]{0,1:T(8,128)} %bitcast.198, f32[40,256]{1,0:T(8,128)} %copy-done.27, pred[256,256]{0,1:T(8,128)(4,1)} %iota_compare_fusion, bf16[256,40,64]{0,2,1:T(8,128)(2,1)} %bitcast.197, bf16[256,40,64]{0,2,1:T(8,128)(2,1)} %bitcast.196), kind=kOutput, calls=%fused_computation.9 | convolution fusion | flops 356429824 | bytes 3203072 | tf_op jit(solution)/shard_map/vmap(thp,shp->hts)/dot_general | solution.py:81
  226.5 1.9 reduce-window.30
  234.0 3.3 copy.265
  237.3 2.6 reduce_sum.150
  242.1 3.3 copy.260
  245.4 2.6 reduce_sum.147
  249.6 2.6 fusion.24
  253.2 104.4 %all-gather.8.cloned.1.call-done = f32[320,64,128]{2,1,0:T(8,128)} async-done(((f32[40,64,128]{2,1,0:T(8,128)}), f32[320,64,128]{2,1,0:T(8,128)}) %all-gather.8.cloned.1.call-update) | async-done | bytes 10485776 | tf_op jit(solution)/shard_map/all_gather | solution.py:21
  357.6 18.2 %while.31 = (s32[]{:T(128)}, f32[1,40,64,128]{3,2,1,0:T(8,128)S(1)}, s32[]{:T(128)}, f32[8,1,40]{2,1,0:T(1,128)}, f32[8,1,40,64,128]{4,3,2,1,0:T(8,128)}, /*index=5*/s32[]{:T(128)}, s32[]{:T(128)}) while((s32[]{:T(128)}, f32[1,40,64,128]{3,2,1,0:T(8,128)S(1)}, s32[]{:T(128)}, f32[8,1,40]{2,1,0:T(1,128)}, ...), condition=%wide.region_6.7_spmd.clone, body=%wide.region_5.6_spmd.clone.sunk | while | flops 1310724 | bytes 3932753 | solution.py:34
  377.2 2.6 fusion.26
  380.9 4.7 %fusion.13 = (f32[2816]{0:T(1024)S(1)}, f32[2816]{0:T(1024)S(1)}, f32[2816]{0:T(1024)S(1)}, f32[2816]{0:T(1024)S(1)}, f32[2816]{0:T(1024)S(1)}, /*index=5*/f32[1,256,2816]{2,1,0:T(8,128)S(1)}) fusion(bf16[1,256,2816]{2,1,0:T(8,128)(2,1)S(1)} %copy-done.4, bf16[1,3,2816]{2,1,0:T(4,128)(2,1)S(1)} %copy-done.20, f32[2816]{0:T(1024)S(1)} %copy-done.13, ...), kind=kLoop, calls=%fused_computation.37 | loop fusion | flops 34588928 | bytes 7338496 | tf_op jit(solution)/shard_map/reduce_sum | solution.py:209
  385.6 2.8 multiply_add_fusion
  388.4 2.9 convert_multiply_fusion.4
  391.3 3.2 copy.255
  394.5 2.1 reduce_sum.145
  402.0 2.0 slice.261
  404.6 41.7 %all-reduce.2 = (f32[4,2816]{1,0:T(4,128)}, f32[2816]{0:T(1024)}, f32[40]{0:T(128)}, f32[40]{0:T(128)}) all-reduce(f32[4,2816]{1,0:T(4,128)S(1)} %pad_maximum_fusion.2, f32[2816]{0:T(1024)S(1)} %get-tuple-element.383, f32[40]{0:T(128)S(1)} %neg.16, f32[40]{0:T(128)S(1)} %reduce_sum.160), channel_id=1, replica_groups=mesh['dp'=4,'seq'=8] {'dp','seq'}, use_global_device_ids=true, to_apply=%region_23.24 | all-reduce | flops 14160 | bytes 113280 | tf_op jit(solution)/shard_map/psum | solution.py:218
  (194 shorter events, 73.7 us)
Async XLA Ops:
  7.2 175.2 %all-gather.6.cloned.1.call-start = ((), (), s32[]{:S(2)}) async-start(), calls=%async_computation | async-start | bytes 11796480 | tf_op jit(solution)/shard_map/all_gather | solution.py:21
  8.0 16.1 %collective-permute-start = (bf16[1,3,2816]{2,1,0:T(4,128)(2,1)S(1)}, bf16[1,3,2816]{2,1,0:T(4,128)(2,1)S(1)}, u32[]{:S(2)}, u32[]{:S(2)}) collective-permute-start(bf16[1,3,2816]{2,1,0:T(4,128)(2,1)S(1)} %slice.105), channel_id=1, source_target_pairs={{0,1},{1,2},{2,3},{3,4},{4,5},{5,6},{6,7},{8,9},{9,10},{10,11},{11... | collective-permute-start | bytes 50696 | tf_op jit(solution)/shard_map/ppermute | solution.py:16
  16.6 3.4 copy-start
  22.0 2.1 copy-start.22
  22.7 5.9 %copy-start.8 = (f32[2816]{0:T(1024)}, f32[2816]{0:T(1024)S(1)}, u32[]{:S(2)}) copy-start(f32[2816]{0:T(1024)S(1)} %get-tuple-element.386) | copy-start | bytes 33796
  22.7 5.9 %copy-start.10 = (f32[2816]{0:T(1024)}, f32[2816]{0:T(1024)S(1)}, u32[]{:S(2)}) copy-start(f32[2816]{0:T(1024)S(1)} %get-tuple-element.388) | copy-start | bytes 33796
  22.7 5.9 %copy-start.12 = (f32[2816]{0:T(1024)}, f32[2816]{0:T(1024)S(1)}, u32[]{:S(2)}) copy-start(f32[2816]{0:T(1024)S(1)} %get-tuple-element.387) | copy-start | bytes 33796
  24.1 5.6 %copy-start.5 = (bf16[2560,256]{1,0:T(8,128)(2,1)S(1)}, bf16[2560,256]{1,0:T(8,128)(2,1)}, u32[]{:S(2)}) copy-start(bf16[2560,256]{1,0:T(8,128)(2,1)} %copy.238) | copy-start | bytes 3932164
  24.2 7.2 %copy-start.19 = (bf16[1,3,2816]{2,1,0:T(4,128)(2,1)}, bf16[1,3,2816]{2,1,0:T(4,128)(2,1)S(1)}, u32[]{:S(2)}) copy-start(bf16[1,3,2816]{2,1,0:T(4,128)(2,1)S(1)} %collective-permute-done) | copy-start | bytes 50692
  31.4 326.2 %all-gather.8.cloned.1.call-start = ((), (), s32[]{:S(2)}) async-start(), calls=%async_computation.1 | async-start | bytes 11796480 | tf_op jit(solution)/shard_map/all_gather | solution.py:21
  62.0 6.7 %copy-start.27 = (f32[40,256]{1,0:T(8,128)}, f32[40,256]{1,0:T(8,128)S(1)}, u32[]{:S(2)}) copy-start(f32[40,256]{1,0:T(8,128)S(1)} %bitcast_add_fusion.3) | copy-start | bytes 122884
  63.1 5.6 %copy-start.6 = (f32[256,256]{1,0:T(8,128)}, f32[256,256]{1,0:T(8,128)S(1)}, u32[]{:S(2)}) copy-start(f32[256,256]{1,0:T(8,128)S(1)} %fusion.35) | copy-start | bytes 786436
  182.3 13.4 %copy-start.24 = (f32[2560]{0:T(1024)S(1)}, f32[2560]{0:T(1024)}, u32[]{:S(2)}) copy-start(f32[2560]{0:T(1024)} %mul.301) | copy-start | bytes 30724
  195.7 9.1 %copy-start.28 = (f32[8,1,40]{2,1,0:T(1,128)}, f32[8,1,40]{2,1,0:T(1,128)S(1)}, u32[]{:S(2)}) copy-start(f32[8,1,40]{2,1,0:T(1,128)S(1)} %get-tuple-element.551) | copy-start | bytes 3844
  206.3 2.4 copy-start.31
  376.3 4.6 %copy-start.3 = (f32[1,256,2560]{2,1,0:T(8,128)S(1)}, f32[1,256,2560]{2,1,0:T(8,128)}, u32[]{:S(2)}) copy-start(f32[1,256,2560]{2,1,0:T(8,128)} %get-tuple-element.419) | copy-start | bytes 7864324
  376.3 4.6 %copy-start.4 = (bf16[1,256,2816]{2,1,0:T(8,128)(2,1)S(1)}, bf16[1,256,2816]{2,1,0:T(8,128)(2,1)}, u32[]{:S(2)}) copy-start(bf16[1,256,2816]{2,1,0:T(8,128)(2,1)} %param.11) | copy-start | bytes 4325380
  376.3 4.6 %copy-start.9 = (f32[2816]{0:T(1024)S(1)}, f32[2816]{0:T(1024)}, u32[]{:S(2)}) copy-start(f32[2816]{0:T(1024)} %copy-done.8) | copy-start | bytes 33796
  376.3 4.6 %copy-start.11 = (f32[2816]{0:T(1024)S(1)}, f32[2816]{0:T(1024)}, u32[]{:S(2)}) copy-start(f32[2816]{0:T(1024)} %copy-done.10) | copy-start | bytes 33796
  376.3 4.6 %copy-start.13 = (f32[2816]{0:T(1024)S(1)}, f32[2816]{0:T(1024)}, u32[]{:S(2)}) copy-start(f32[2816]{0:T(1024)} %copy-done.12) | copy-start | bytes 33796
  376.3 4.6 %copy-start.20 = (bf16[1,3,2816]{2,1,0:T(4,128)(2,1)S(1)}, bf16[1,3,2816]{2,1,0:T(4,128)(2,1)}, u32[]{:S(2)}) copy-start(bf16[1,3,2816]{2,1,0:T(4,128)(2,1)} %copy-done.19) | copy-start | bytes 50692
  376.3 4.6 %copy-start.23 = (f32[2816]{0:T(1024)S(1)}, f32[2816]{0:T(1024)}, u32[]{:S(2)}) copy-start(f32[2816]{0:T(1024)} %param.13) | copy-start | bytes 33796
  394.5 2.3 copy-start.7
  394.5 2.3 copy-start.30
  394.5 4.3 copy-start.25
  394.5 6.5 %copy-start.21 = (f32[40,2]{1,0:T(8,128)S(1)}, f32[40,2]{1,0:T(8,128)}, u32[]{:S(2)}) copy-start(f32[40,2]{1,0:T(8,128)} %copy.254) | copy-start | bytes 964
  394.5 6.7 %copy-start.14 = (f32[1,40,256]{2,1,0:T(8,128)S(1)}, f32[1,40,256]{2,1,0:T(8,128)}, u32[]{:S(2)}) copy-start(f32[1,40,256]{2,1,0:T(8,128)} %param.14) | copy-start | bytes 122884
  394.5 6.7 %copy-start.15 = (f32[1,40,2,128]{3,2,0,1:T(2,128)S(1)}, f32[1,40,2,128]{3,2,0,1:T(2,128)}, u32[]{:S(2)}) copy-start(f32[1,40,2,128]{3,2,0,1:T(2,128)} %copy.253) | copy-start | bytes 122884
  394.5 6.7 %copy-start.17 = (f32[40,256]{1,0:T(8,128)S(1)}, f32[40,256]{1,0:T(8,128)}, u32[]{:S(2)}) copy-start(f32[40,256]{1,0:T(8,128)} %copy-done.16) | copy-start | bytes 122884
  394.5 6.7 %copy-start.18 = (f32[256,40]{0,1:T(8,128)S(1)}, f32[256,40]{0,1:T(8,128)}, u32[]{:S(2)}) copy-start(f32[256,40]{0,1:T(8,128)} %reduce_sum.150) | copy-start | bytes 122884
  394.5 7.3 %copy-start.32 = (f32[40]{0:T(128)S(1)}, f32[40]{0:T(128)}, u32[]{:S(2)}) copy-start(f32[40]{0:T(128)} %neg.15) | copy-start | bytes 484
  398.8 47.4 %collective-permute-start.1 = (f32[1,3,2816]{2,1,0:T(4,128)S(1)}, f32[1,3,2816]{2,1,0:T(4,128)S(1)}, u32[]{:S(2)}, u32[]{:S(2)}) collective-permute-start(f32[1,3,2816]{2,1,0:T(4,128)S(1)} %fusion.46), channel_id=1, source_target_pairs={{1,0},{2,1},{3,2},{4,3},{5,4},{6,5},{7,6},{9,8},{10,9},{11,10},{12... | collective-permute-start | bytes 101384 | tf_op jit(solution)/shard_map/ppermute | solution.py:16
  (6 other events, 7.2 us)
Sparse Core Ops, SparseCore 0:
  31.6 150.7 all-gather.5
  208.9 148.6 all-gather.7
where the time goes:
time: 457 us; the launch traced here: 455 us
  waiting for transfers between devices  215 us (47%)
  local copies, waits for them, and re-layouts  61.2 us (13%)
  blocking collectives  60.8 us (13%)
  other arithmetic  59.6 us (13%)
  matrix products  37.2 us (8%)
  between operations  14.8 us (3%)
  starting transfers between devices  6.27 us (1%)
    all_gather x2, waiting for transfers between devices, carried_in(): everything = jax.tree.map(lambda part: lax.all_gather(part, axis), array)  215 us
    psum x1, blocking collectives, shards(): lax.psum((local_weight, local_bias, local_rates, local_skip), ('dp', 'seq'))  41.7 us
    select_n x16, other arithmetic, lap(): return jax.tree.map(lambda a, b: jnp.where(reached, a, b), new, before)  25.9 us
    all_gather x1, blocking collectives, carried_in(): everything = jax.tree.map(lambda part: lax.all_gather(part, axis), array)  19.1 us
  transfers between devices with their start and end apart: 4, of which 2 were waited for; matrix products, arithmetic and copies ran while one was open for 18% of the time, Pallas kernels for 0%

commit v1 on v0

v1 whole, which is shorter than its diff:
```python
import functools
import jax
import jax.numpy as jnp
from jax import lax
from jax.experimental import pallas as pl
from jax.experimental.pallas import tpu as pltpu
from jax.sharding import PartitionSpec as P

HEADS = 40
HEAD_DIM = 64
STATE = 128
GROUP = 256
KCONV = 4
XW = HEADS * HEAD_DIM
CH = XW + 2 * STATE
TILE = 256
HALF = HEADS // 2
CHUNK = 5
NCHUNK = HALF // CHUNK
MESH = pl.DeviceIdType.MESH
F32 = jnp.float32
BF16 = jnp.bfloat16
HI = lax.Precision.HIGHEST
VM = functools.partial(pl.BlockSpec, memory_space=pltpu.VMEM)
SM = functools.partial(pl.BlockSpec, memory_space=pltpu.SMEM)


def dot(a, b, ca, cb):
    return lax.dot_general(a, b, (((ca,), (cb,)), ((), ())), preferred_element_type=F32)


def shifted(array, axis, by):
    length = lax.axis_size(axis)
    pairs = [(i, i + by) for i in range(length) if 0 <= i + by < length]
    return lax.ppermute(array, axis, pairs)


def locals_kernel(
    xbc_ref, before_ref, w_ref, bias_ref, step_ref, rate_ref, dy_ref,
    zt_ref, bc_ref, dyt_ref, der_ref, cl_ref, s_ref, u_ref, end_ref, xw_ref, dw_ref,
):
    row = lax.broadcasted_iota(jnp.int32, (GROUP, GROUP), 0)
    col = lax.broadcasted_iota(jnp.int32, (GROUP, GROUP), 1)
    upper = (row <= col).astype(F32)
    log_steps = -(step_ref[...] * rate_ref[...])
    cl_ref[...] = jnp.dot(log_steps, upper, precision=HI, preferred_element_type=F32)

    def activate(cols):
        x = xbc_ref[:, cols].astype(F32)
        padded = jnp.concatenate([before_ref[:, cols].astype(F32), x], axis=0)
        pre = bias_ref[:, cols]
        for k in range(KCONV):
            pre = pre + w_ref[k : k + 1, cols] * padded[5 + k : 5 + k + GROUP]
        sig = 1.0 / (1.0 + jnp.exp(-pre))
        der_ref[:, cols] = sig * (1.0 + pre * (1.0 - sig))
        return pre * sig

    @pl.loop(0, XW // TILE)
    def _(i):
        cols = pl.ds(pl.multiple_of(i * TILE, TILE), TILE)
        zt_ref[cols, :] = activate(cols).T.astype(BF16)
        dyt_ref[cols, :] = dy_ref[:, cols].astype(F32).T.astype(BF16)

    tail_z = activate(pl.ds(XW, TILE))
    bc_ref[...] = tail_z.astype(BF16)
    zt_ref[pl.ds(XW, TILE), :] = tail_z.T.astype(BF16)
    cum = cl_ref[...]
    end_ref[...] = jnp.broadcast_to(jnp.exp(cum[:, GROUP - 1 : GROUP]), (HEADS, STATE))

    @pl.loop(0, HEADS)
    def _(h):
        rows = pl.ds(pl.multiple_of(h * HEAD_DIM, HEAD_DIM), HEAD_DIM)
        cl = cl_ref[pl.ds(h, 1), :]
        xw_ref[rows, :] = (
            zt_ref[rows, :].astype(F32) * jnp.exp(cl[:, GROUP - 1 : GROUP] - cl)
        ).astype(BF16)
        dw_ref[rows, :] = (dyt_ref[rows, :].astype(F32) * jnp.exp(cl)).astype(BF16)

    @pl.loop(0, XW // TILE)
    def _(i):
        rows = pl.ds(pl.multiple_of(i * TILE, TILE), TILE)
        s_ref[rows, :] = dot(xw_ref[rows, :], bc_ref[:, :STATE], 1, 0).astype(BF16)
        u_ref[rows, :] = dot(dw_ref[rows, :], bc_ref[:, STATE:], 1, 0).astype(BF16)


def states_kernel(
    s_ref, u_ref, a_ref, start_ref, end_ref,
    sp, up, ap, ein, gin, eout, gout, sout, uout,
    send1, recv1, send2, recv2, send3, recv3, senda, recva,
):
    me = lax.axis_index("seq")
    n = lax.axis_size("seq")
    y = me % 2
    z = me // 2
    nz = n // 2
    pair = me + 1 - 2 * y
    mine = y * HALF
    other = (1 - y) * HALF
    last = nz - 1

    barrier = pltpu.get_barrier_semaphore()
    pl.semaphore_signal(barrier, inc=1, device_id={"seq": pair}, device_id_type=MESH)

    @pl.when(z > 0)
    def _():
        pl.semaphore_signal(barrier, inc=1, device_id={"seq": me - 2}, device_id_type=MESH)

    @pl.when(z < last)
    def _():
        pl.semaphore_signal(barrier, inc=1, device_id={"seq": me + 2}, device_id_type=MESH)

    edge = jnp.where(z > 0, 1, 0) + jnp.where(z < last, 1, 0)
    pl.semaphore_wait(barrier, 1 + edge)

    def send(src, dst, ss, rs, to):
        return pltpu.make_async_remote_copy(
            src_ref=src, dst_ref=dst, send_sem=ss, recv_sem=rs,
            device_id={"seq": to}, device_id_type=MESH,
        )

    def part(c):
        return pl.ds(c * CHUNK, CHUNK)

    def pair_copy(j, c):
        src, dst = ((s_ref, sp), (u_ref, up))[j]
        return send(
            src.at[pl.ds(other + c * CHUNK, CHUNK)], dst.at[part(c)],
            send1.at[j, c], recv1.at[j, c], pair,
        )

    def chain_copy(j, c):
        src, dst = ((eout, ein), (gout, gin))[j]
        return send(
            src.at[part(c)], dst.at[part(c)], send2.at[j, c], recv2.at[j, c],
            me + 2 if j == 0 else me - 2,
        )

    def back_copy(j, c):
        src, dst = ((sout, start_ref), (uout, end_ref))[j]
        return send(
            src.at[part(c)], dst.at[pl.ds(mine + c * CHUNK, CHUNK)],
            send3.at[j, c], recv3.at[j, c], pair,
        )

    decay_copy = send(a_ref, ap, senda, recva, pair)
    decay_copy.start()

    def begin(j):
        @pl.loop(0, NCHUNK)
        def _(c):
            pair_copy(j, c).start()

    def run(j):
        has_in = z > 0 if j == 0 else z < last
        has_out = z < last if j == 0 else z > 0
        inbox, outbox = ((ein, eout), (gin, gout))[j]
        got, own, back, result = ((sp, s_ref, sout, start_ref), (up, u_ref, uout, end_ref))[j]

        @pl.when(jnp.logical_not(has_in))
        def _():
            inbox[...] = jnp.zeros_like(inbox)

        @pl.loop(0, NCHUNK)
        def _(c):
            pair_copy(j, c).wait_recv()
            here = pl.ds(mine + c * CHUNK, CHUNK)
            first = y == 0
            aa = a_ref[here, :][:, None, :]
            bb = ap[here, :][:, None, :]
            a0 = jnp.where(first, aa, bb)
            a1 = jnp.where(first, bb, aa)
            vv = own[here].astype(F32)
            ww = got[part(c)].astype(F32)
            v0 = jnp.where(first, vv, ww)
            v1 = jnp.where(first, ww, vv)

            @pl.when(has_in)
            def _():
                chain_copy(j, c).wait_recv()

            carry = inbox[part(c)].astype(F32)
            if j == 0:
                near, far = carry, a0 * carry + v0
                leave = a1 * far + v1
                kept = jnp.where(first, near, far)
                given = jnp.where(first, far, near)
            else:
                far, near = carry, a1 * carry + v1
                leave = a0 * near + v0
                kept = jnp.where(first, near, far)
                given = jnp.where(first, far, near)
            outbox[part(c)] = leave.astype(BF16)

            @pl.when(has_out)
            def _():
                chain_copy(j, c).start()

            back[part(c)] = given.astype(BF16)
            back_copy(j, c).start()
            result[here] = kept.astype(BF16)

    @pl.when(z < nz - nz // 2)
    def _():
        begin(0)
        begin(1)
        decay_copy.wait_recv()
        run(0)
        run(1)

    @pl.when(z >= nz - nz // 2)
    def _():
        begin(1)
        begin(0)
        decay_copy.wait_recv()
        run(1)
        run(0)

    decay_copy.wait_send()
    for j in range(2):
        @pl.loop(0, NCHUNK)
        def _(c):
            pair_copy(j, c).wait_send()
            back_copy(j, c).wait()

            @pl.when(z < last if j == 0 else z > 0)
            def _():
                chain_copy(j, c).wait_send()


def grads_kernel(
    zt_ref, bc_ref, dyt_ref, der_ref, cl_ref, s_ref, a_ref, xw_ref, dw_ref,
    step_ref, rate_ref, skip_ref, xbc_ref, before_ref, w_ref,
    gin_ref, edge_ref, front_ref, gstep_ref, gw_ref, grate_ref, gskip_ref,
    gz_ref, wsum_ref, d_ref, q_ref, l_ref, k_ref,
):
    row = lax.broadcasted_iota(jnp.int32, (GROUP, GROUP), 0)
    col = lax.broadcasted_iota(jnp.int32, (GROUP, GROUP), 1)
    causal = row >= col
    bproj = bc_ref[:, :STATE]
    cproj = bc_ref[:, STATE:]
    gram = dot(cproj, bproj, 1, 1)
    wsum_ref[...] = jnp.zeros_like(wsum_ref)

    def head(h):
        rows = pl.ds(pl.multiple_of(h * HEAD_DIM, HEAD_DIM), HEAD_DIM)
        xt = zt_ref[rows, :]
        dyt = dyt_ref[rows, :]
        cl = cl_ref[pl.ds(h, 1), :]
        wide = jnp.broadcast_to(cl, (STATE, GROUP)).T
        gap = jnp.concatenate([wide, wide], axis=1) - cl
        decay = jnp.where(causal, jnp.exp(gap), 0.0)
        inner = dot(dyt, xt, 0, 0)
        wsum_ref[...] += decay * inner
        kmat = (decay * gram).astype(BF16)
        intra = dot(dyt, kmat, 1, 0)
        yt = dot(xt, kmat, 1, 1)
        badj = dot(a_ref[rows, :], zt_ref[pl.ds(XW, STATE), :], 1, 0)
        cst = dot(s_ref[rows, :], zt_ref[pl.ds(XW + STATE, STATE), :], 1, 0)
        log_end = cl[:, GROUP - 1 : GROUP]
        tail = jnp.exp(log_end - cl)
        xf = xt.astype(F32)
        dyf = dyt.astype(F32)
        csum = jnp.sum(xf * intra, axis=0, keepdims=True)
        rsum = jnp.sum(dyf * yt, axis=0, keepdims=True)
        rterm = tail * jnp.sum(xf * badj, axis=0, keepdims=True)
        qterm = jnp.exp(cl) * jnp.sum(dyf * cst, axis=0, keepdims=True)
        prod = a_ref[rows, :].astype(F32) * s_ref[rows, :].astype(F32)
        four = jnp.exp(log_end) * jnp.sum(jnp.sum(prod, axis=0, keepdims=True), axis=1, keepdims=True)
        one = pl.ds(h, 1)
        gain = csum - rsum + rterm
        d_ref[one, :] = gain
        q_ref[one, :] = qterm
        l_ref[one, :] = four - gain
        k_ref[one, :] = jnp.sum(xf * dyf, axis=0, keepdims=True)
        return intra + tail * badj + skip_ref[h] * dyf

    @pl.loop(0, HEADS // 2)
    def _(hp):
        both = jnp.concatenate([head(2 * hp), head(2 * hp + 1)], axis=0)
        gz_ref[:, pl.ds(pl.multiple_of(hp * STATE, STATE), STATE)] = both.T

    wlow = wsum_ref[...].astype(BF16)
    gb = dot(wlow, cproj, 0, 0) + dot(a_ref[...], xw_ref[...], 0, 0).T
    gc = dot(wlow, bproj, 1, 0) + dot(s_ref[...], dw_ref[...], 0, 0).T
    gz_ref[:, pl.ds(XW, STATE)] = gb
    gz_ref[:, pl.ds(XW + STATE, STATE)] = gc
    upper = (row <= col).astype(F32)
    lower = (row >= col).astype(F32)
    glog = jnp.dot(d_ref[...], upper, precision=HI, preferred_element_type=F32)
    glog = glog + jnp.dot(q_ref[...], lower, precision=HI, preferred_element_type=F32)
    glog = glog + l_ref[...]
    gstep_ref[...] = -rate_ref[...] * glog
    grate_ref[...] = -jnp.sum(step_ref[...] * glog, axis=1, keepdims=True)
    gskip_ref[...] = jnp.sum(k_ref[...], axis=1, keepdims=True)

    @pl.loop(0, CH // TILE)
    def _(i):
        cols = pl.ds(pl.multiple_of(i * TILE, TILE), TILE)
        gp = gz_ref[:, cols] * der_ref[:, cols]
        padded = jnp.concatenate([gp, jnp.zeros((8, TILE), F32)], axis=0)
        gin = w_ref[KCONV - 1 : KCONV, cols] * gp
        for k in range(KCONV - 1):
            off = KCONV - 1 - k
            gin = gin + w_ref[k : k + 1, cols] * padded[off : off + GROUP]
        gin_ref[:, cols] = gin.astype(BF16)
        edge_ref[:, cols] = gin[GROUP - 8 :]
        first = gp[:8]
        sub = lax.broadcasted_iota(jnp.int32, (8, TILE), 0)
        front_pad = jnp.concatenate([jnp.zeros((8, TILE), F32), first], axis=0)
        rim = jnp.zeros((8, TILE), F32)
        for k in range(KCONV - 1):
            off = KCONV - 1 - k
            piece = jnp.where(sub >= 8 - off, front_pad[off : off + 8], 0.0)
            rim = rim + w_ref[k : k + 1, cols] * piece
        front_ref[:, cols] = rim
        x = jnp.concatenate([before_ref[:, cols].astype(F32), xbc_ref[:, cols].astype(F32)], axis=0)
        for k in range(KCONV):
            gw_ref[k : k + 1, cols] = jnp.sum(gp * x[5 + k : 5 + k + GROUP], axis=0, keepdims=True)
        gw_ref[KCONV : KCONV + 1, cols] = jnp.sum(gp, axis=0, keepdims=True)


def bits_of(n):
    out = []
    b = 1
    while b < n:
        out.append(b)
        b *= 2
    return out


def reduce_kernel(steps, pack_ref, front_ref, out_ref, rim_ref, acc, box, ssem, rsem, fs, fr):
    pos = {"dp": lax.axis_index("dp"), "seq": lax.axis_index("seq")}
    n = lax.axis_size("seq")
    me = pos["seq"]
    to = []
    for axis, b in steps:
        p = pos[axis]
        to.append({axis: p + b * (1 - 2 * ((p // b) % 2))})
    barrier = pltpu.get_barrier_semaphore()
    for where in to:
        pl.semaphore_signal(barrier, inc=1, device_id=where, device_id_type=MESH)

    @pl.when(me > 0)
    def _():
        pl.semaphore_signal(barrier, inc=1, device_id={"seq": me - 1}, device_id_type=MESH)

    @pl.when(me < n - 1)
    def _():
        pl.semaphore_signal(barrier, inc=1, device_id={"seq": me + 1}, device_id_type=MESH)

    edge = jnp.where(me > 0, 1, 0) + jnp.where(me < n - 1, 1, 0)
    pl.semaphore_wait(barrier, len(to) + edge)

    rim = pltpu.make_async_remote_copy(
        src_ref=front_ref, dst_ref=rim_ref, send_sem=fs, recv_sem=fr,
        device_id={"seq": me - 1}, device_id_type=MESH,
    )

    @pl.when(me > 0)
    def _():
        rim.start()

    copies = []
    for i, where in enumerate(to):
        copy = pltpu.make_async_remote_copy(
            src_ref=pack_ref if i == 0 else acc.at[i], dst_ref=box.at[i],
            send_sem=ssem.at[i], recv_sem=rsem.at[i],
            device_id=where, device_id_type=MESH,
        )
        copy.start()
        copies.append(copy)
        copy.wait_recv()
        total = (pack_ref[...] if i == 0 else acc[i]) + box[i]
        if i + 1 < len(to):
            acc[i + 1] = total
        else:
            out_ref[...] = total
    for copy in copies:
        copy.wait_send()

    @pl.when(me > 0)
    def _():
        rim.wait_send()

    @pl.when(me < n - 1)
    def _():
        rim.wait_recv()

    @pl.when(me == n - 1)
    def _():
        rim_ref[...] = jnp.zeros_like(rim_ref)


def sds(shape, dtype):
    return jax.ShapeDtypeStruct(shape, dtype)


LIMIT = 60 * 1024 * 1024


def shards(xbc_in, conv_weight, conv_bias, step_sizes, decay_rates, skip_gain, grad_out):
    rim_len = KCONV - 1
    tokens = xbc_in.shape[1]
    before = shifted(xbc_in[:, tokens - 8 :, :], "seq", 1)[0]
    xbc = xbc_in[0]
    dy = grad_out[0]
    step = step_sizes[0]
    rate = decay_rates[:, None]
    state = (HEADS, HEAD_DIM, STATE)
    zt, bc, dyt, der, cl, s, u, decay, xw, dw = pl.pallas_call(
        locals_kernel,
        out_shape=[
            sds((CH, GROUP), BF16), sds((GROUP, 2 * STATE), BF16), sds((XW, GROUP), BF16),
            sds((GROUP, CH), F32), sds((HEADS, GROUP), F32), sds((XW, STATE), BF16),
            sds((XW, STATE), BF16), sds((HEADS, STATE), F32), sds((XW, GROUP), BF16),
            sds((XW, GROUP), BF16),
        ],
        in_specs=[VM()] * 7,
        out_specs=[VM()] * 10,
        compiler_params=pltpu.CompilerParams(vmem_limit_bytes=LIMIT),
    )(xbc, before, conv_weight, conv_bias[None], step, rate, dy)

    half = (HALF, HEAD_DIM, STATE)
    dma = pltpu.SemaphoreType.DMA
    start, end = pl.pallas_call(
        states_kernel,
        out_shape=[sds(state, BF16)] * 2,
        in_specs=[VM()] * 3,
        out_specs=[VM()] * 2,
        scratch_shapes=[pltpu.VMEM(half, BF16)] * 2
        + [pltpu.VMEM((HEADS, STATE), F32)]
        + [pltpu.VMEM(half, BF16)] * 6
        + [dma((2, NCHUNK))] * 6
        + [dma, dma],
        compiler_params=pltpu.CompilerParams(
            vmem_limit_bytes=LIMIT, collective_id=0, has_side_effects=True
        ),
    )(s.reshape(state), u.reshape(state), decay)

    gin, edge, front, gstep, gw, grate, gskip = pl.pallas_call(
        grads_kernel,
        out_shape=[
            sds((GROUP, CH), BF16), sds((8, CH), F32), sds((8, CH), F32), sds((HEADS, GROUP), F32),
            sds((KCONV + 1, CH), F32), sds((HEADS, 1), F32), sds((HEADS, 1), F32),
        ],
        in_specs=[VM()] * 11 + [SM()] + [VM()] * 3,
        out_specs=[VM()] * 7,
        scratch_shapes=[pltpu.VMEM((GROUP, CH), F32), pltpu.VMEM((GROUP, GROUP), F32)]
        + [pltpu.VMEM((HEADS, GROUP), F32)] * 4,
        compiler_params=pltpu.CompilerParams(vmem_limit_bytes=LIMIT),
    )(
        zt, bc, dyt, der, cl, start.reshape(XW, STATE), end.reshape(XW, STATE), xw, dw,
        step, rate, skip_gain, xbc, before, conv_weight,
    )

    small = jnp.concatenate([grate[:, 0], gskip[:, 0], jnp.zeros((CH - 2 * HEADS,), F32)])
    pack = jnp.concatenate([gw, small[None], jnp.zeros((2, CH), F32)], axis=0)
    steps = [("dp", b) for b in bits_of(lax.axis_size("dp"))]
    steps += [("seq", b) for b in bits_of(lax.axis_size("seq"))]
    count = len(steps)
    total, rim = pl.pallas_call(
        functools.partial(reduce_kernel, steps),
        out_shape=[sds((8, CH), F32)] * 2,
        in_specs=[VM()] * 2,
        out_specs=[VM()] * 2,
        scratch_shapes=[pltpu.VMEM((count, 8, CH), F32)] * 2 + [dma((count,))] * 2 + [dma, dma],
        compiler_params=pltpu.CompilerParams(
            vmem_limit_bytes=LIMIT, collective_id=1, has_side_effects=True
        ),
    )(pack, front)
    final = (edge + rim).astype(BF16)
    grad_in = lax.dynamic_update_slice(gin, final, (tokens - 8, 0))
    return (
        grad_in[None], gstep[None], total[:KCONV], total[KCONV],
        total[KCONV + 1, :HEADS], total[KCONV + 1, HEADS : 2 * HEADS],
    )


def solution(mesh):
    return jax.shard_map(
        shards,
        mesh=mesh,
        in_specs=(
            P("dp", "seq", None), P(), P(), P("dp", None, "seq"), P(), P(), P("dp", "seq", None),
        ),
        out_specs=(P("dp", "seq", None), P("dp", None, "seq"), P(), P(), P(), P()),
        check_vma=False,
    )
```

time: 457 us -> 110 us (0.24)
  waiting for transfers between devices: 215 us -> 0.01 us
  Pallas kernels: 0 us -> 90.6 us
  blocking collectives: 60.8 us -> 0 us
  other arithmetic: 59.6 us -> 4.83 us
  local copies, waits for them, and re-layouts: 61.2 us -> 8.61 us
  matrix products: 37.2 us -> 0 us
  between operations: 14.8 us -> 0.67 us
    all_gather x2 -> x0, waiting for transfers between devices: 215 us -> none  [carried_in(): everything = jax.tree.map(lambda part: lax.all_gather(part, axis), array)]
    pallas_call x0 -> x4, Pallas kernels: none -> 90.6 us  [the longest x1 34.6 us: shards(): pl.pallas_call(states_kernel, out_shape=[sds(state, BF16)] * 2, in_specs=...]
    psum x1 -> x0, blocking collectives: 41.7 us -> none  [shards(): lax.psum((local_weight, local_bias, local_rates, local_skip), ('dp', 'seq'))]
    dot_general x11 -> x0, matrix products: 37.2 us -> none  [the longest x1 8.95 us: block_grads(): lax.dot_general(b_proj, adjoint_low, contract_last, preferred_element_typ...]
    select_n x16 -> x0, other arithmetic: 25.9 us -> none  [lap(): return jax.tree.map(lambda a, b: jnp.where(reached, a, b), new, before)]
    all_gather x1 -> x0, blocking collectives: 19.1 us -> none  [carried_in(): everything = jax.tree.map(lambda part: lax.all_gather(part, axis), array)]
    mul x20 -> x0, local copies, waits for them, and re-layouts: 15.6 us -> none  [the longest x16 5.14 us: compose(): later[0][:, :, None, None] * earlier[1] + later[1]]
    reduce_sum x7 -> x0, other arithmetic: 14 us -> none  [the longest x1 4.65 us: shards(): jnp.sum(grad_pre * padded_in[:, tap_index:tap_index + tokens].astype(jnp....]
  transfers between devices with their start and end apart: 4 -> 1, of which waited for: 2 -> 0; matrix products, arithmetic and copies ran while one was open for 18% -> 2% of each run, Pallas kernels for 0% -> 0%
where the time goes in v1:
time: 110 us
  Pallas kernels  90.6 us (82%)
  local copies, waits for them, and re-layouts  8.61 us (8%)
  starting transfers between devices  4.89 us (4%)
  other arithmetic  4.83 us (4%)
    pallas_call x1, Pallas kernels, shards(): pl.pallas_call(states_kernel, out_shape=[sds(state, BF16)] * 2, in_specs=...  34.6 us
    pallas_call x1, Pallas kernels, shards(): pl.pallas_call(functools.partial(reduce_kernel, steps), out_shape=[sds((8...  21.1 us
    pallas_call x1, Pallas kernels, shards(): pl.pallas_call(grads_kernel, out_shape=[sds((GROUP, CH), BF16), sds((8, C...  19.2 us
    pallas_call x1, Pallas kernels, shards(): pl.pallas_call(locals_kernel, out_shape=[sds((CH, GROUP), BF16), sds((GRO...  15.7 us
    ppermute x1, starting transfers between devices, shifted(): return lax.ppermute(array, axis, pairs)  4.89 us
  transfers between devices with their start and end apart: 1, of which 0 were waited for; matrix products, arithmetic and copies ran while one was open for 2% of the time, Pallas kernels for 0%

profile of v1, /device:TPU:0, one launch (start us, length us, event | category | flops | bytes accessed | tf_op | source)
XLA Modules:
  0.0 109.6 jit_solution(10442182648598125627)
XLA Ops:
  0.6 0.8 slice.15
  1.4 4.9 %collective-permute-start = (bf16[1,8,2816]{2,1,0:T(8,128)(2,1)S(1)}, bf16[1,8,2816]{2,1,0:T(8,128)(2,1)S(1)}, u32[]{:S(2)}, u32[]{:S(2)}) collective-permute-start(bf16[1,8,2816]{2,1,0:T(8,128)(2,1)S(1)} %slice.15), channel_id=1, source_target_pairs={{0,1},{1,2},{2,3},{3,4},{4,5},{5,6},{6,7},{8,9},{9,10},{10,11},{11... | collective-permute-start | bytes 135176 | tf_op jit(solution)/shard_map/ppermute | solution.py:35
  6.3 1.3 %copy.15.rate_ref = f32[40,1]{1,0:T(8,128)} copy(f32[40,1]{0,1:T(1,128)} %bitcast.30) | data formatting | bytes 320 | tf_op jit(solution)/shard_map/broadcast_in_dim | solution.py:408
  7.7 1.3 %broadcast_in_dim.23.bias_ref = f32[1,2816]{1,0:T(1,128)} reshape(f32[2816]{0:T(1024)} %param.9) | data formatting | bytes 22528 | tf_op jit(solution)/shard_map/broadcast_in_dim | solution.py:421
  9.0 0.1 pad.2.clone
  9.1 0.0 collective-permute-done
  9.1 0.0 copy-start
  9.1 0.6 copy-done
  9.7 15.7 %shard_map.118 = (bf16[2816,256]{1,0:T(8,128)(2,1)}, bf16[256,256]{1,0:T(8,128)(2,1)}, bf16[2560,256]{1,0:T(8,128)(2,1)}, f32[256,2816]{1,0:T(8,128)}, f32[40,25...) custom-call(bf16[256,2816]{1,0:T(8,128)(2,1)} %bitcast.19, ...), custom_call_target="tpu_custom_call" | custom-call | tf_op jit(solution)/shard_map/pallas_call | solution.py:410
  25.4 34.6 %shard_map.119 = (bf16[40,64,128]{2,1,0:T(8,128)(2,1)}, bf16[40,64,128]{2,1,0:T(8,128)(2,1)}) custom-call(bf16[40,64,128]{2,1,0:T(8,128)(2,1)} %bitcast.24, bf16[40,64,128]{2,1,0:T(8,128)(2,1)} %bitcast.25, f32[40,128]{1,0:T(8,128)} %get-tuple-element.34.a_ref), custom_call_target="tpu_custom_call" | custom-call | tf_op jit(solution)/shard_map/pallas_call | solution.py:425
  60.0 19.2 %shard_map.120 = (bf16[256,2816]{1,0:T(8,128)(2,1)}, f32[8,2816]{1,0:T(8,128)}, f32[8,2816]{1,0:T(8,128)}, f32[40,256]{1,0:T(8,128)}, f32[5,2816]{1,0:T(8,128)}, /*index=5*/f32[40,1]{1,0:T(8,128)}, f32[40,1]{1,0:T(8,128)}) custom-call(bf16[2816,256]{1,0:T(8,128)(2,1)} %get-tuple-element.27.zt_ref, bf16[256,256]{1,0:T(8,128)(2,1)} %get-tuple-element.28.bc_ref, ...), custom_call_target="tpu_custom_call" | custom-call | tf_op jit(solution)/shard_map/pallas_call | solution.py:440
  79.2 0.8 reduce
  80.0 0.8 reduce.1
  80.9 0.1 concatenate.6
  81.0 1.6 %maximum_maximum_fusion.pack_ref = f32[8,2816]{1,0:T(8,128)} fusion(f32[1,2816]{1,0:T(1,128)S(1)} %broadcast_in_dim.27, f32[5,2816]{1,0:T(8,128)} %get-tuple-element.41, f32[8]{0:T(128)S(1)} %pad.2.clone), kind=kLoop, calls=%fused_computation | loop fusion | flops 45056 | bytes 157728 | tf_op jit(solution)/shard_map/concatenate | solution.py:457
  82.6 21.1 %shard_map.121 = (f32[8,2816]{1,0:T(8,128)}, f32[8,2816]{1,0:T(8,128)}) custom-call(f32[8,2816]{1,0:T(8,128)} %maximum_maximum_fusion.pack_ref, f32[8,2816]{1,0:T(8,128)} %get-tuple-element.44.front_ref), custom_call_target="tpu_custom_call" | custom-call | tf_op jit(solution)/shard_map/pallas_call | solution.py:461
  103.7 1.5 %slice.16 = f32[4,2816]{1,0:T(4,128)} slice(f32[8,2816]{1,0:T(8,128)} %get-tuple-element.47), slice={[0:4], [0:2816]} | slice | bytes 90112 | tf_op jit(solution)/shard_map/slice | solution.py:474
  105.2 1.5 %slice_reduce_fusion = f32[2816]{0:T(1024)} fusion(f32[8,2816]{1,0:T(8,128)} %get-tuple-element.47), kind=kLoop, calls=%fused_computation.4 | loop fusion | bytes 22528 | tf_op jit(solution)/shard_map/slice | solution.py:474
  106.7 1.3 %slice_bitcast_fusion = (f32[40]{0:T(128)}, f32[40]{0:T(128)}) fusion(f32[8,2816]{1,0:T(8,128)} %get-tuple-element.47), kind=kLoop, calls=%fused_computation.5 | loop fusion | bytes 640 | tf_op jit(solution)/shard_map/squeeze | solution.py:475
  108.1 1.6 %fusion.1 = bf16[1,256,2816]{2,1,0:T(8,128)(2,1)} fusion(bf16[1,256,2816]{2,1,0:T(8,128)(2,1)} %bitcast.31, f32[8,2816]{1,0:T(8,128)} %get-tuple-element.40, f32[8,2816]{1,0:T(8,128)} %get-tuple-element.45), kind=kLoop, calls=%fused_computation.3 | loop fusion | flops 45056 | bytes 225280 | tf_op jit(solution)/shard_map/dynamic_update_slice | solution.py:472
  (3 shorter events, 0.0 us)
Async XLA Ops:
  1.4 7.6 %collective-permute-start = (bf16[1,8,2816]{2,1,0:T(8,128)(2,1)S(1)}, bf16[1,8,2816]{2,1,0:T(8,128)(2,1)S(1)}, u32[]{:S(2)}, u32[]{:S(2)}) collective-permute-start(bf16[1,8,2816]{2,1,0:T(8,128)(2,1)S(1)} %slice.15), channel_id=1, source_target_pairs={{0,1},{1,2},{2,3},{3,4},{4,5},{5,6},{6,7},{8,9},{9,10},{10,11},{11... | collective-permute-start | bytes 135176 | tf_op jit(solution)/shard_map/ppermute | solution.py:35
  9.1 0.6 copy-start

commit v2 on v1

--- a/solution.py
+++ b/solution.py
@@ -16,6 +16,9 @@
 TILE = 256
 HALF = HEADS // 2
 CHUNK = 5
+EDGE = 16
+LINES = CH // TILE
+PACK = (KCONV + 1) * LINES + 1
 NCHUNK = HALF // CHUNK
 MESH = pl.DeviceIdType.MESH
 F32 = jnp.float32
@@ -38,17 +41,23 @@
 def locals_kernel(
     xbc_ref, before_ref, w_ref, bias_ref, step_ref, rate_ref, dy_ref,
     zt_ref, bc_ref, dyt_ref, der_ref, cl_ref, s_ref, u_ref, end_ref, xw_ref, dw_ref,
+    log_ref,
 ):
     row = lax.broadcasted_iota(jnp.int32, (GROUP, GROUP), 0)
     col = lax.broadcasted_iota(jnp.int32, (GROUP, GROUP), 1)
     upper = (row <= col).astype(F32)
-    log_steps = -(step_ref[...] * rate_ref[...])
-    cl_ref[...] = jnp.dot(log_steps, upper, precision=HI, preferred_element_type=F32)
+
+    @pl.loop(0, HEADS)
+    def _(h):
+        one = pl.ds(h, 1)
+        log_ref[one, :] = -(step_ref[one, :] * rate_ref[h])
+
+    cl_ref[...] = jnp.dot(log_ref[...], upper, precision=HI, preferred_element_type=F32)
 
     def activate(cols):
         x = xbc_ref[:, cols].astype(F32)
         padded = jnp.concatenate([before_ref[:, cols].astype(F32), x], axis=0)
-        pre = bias_ref[:, cols]
+        pre = bias_ref[cols][None, :]
         for k in range(KCONV):
             pre = pre + w_ref[k : k + 1, cols] * padded[5 + k : 5 + k + GROUP]
         sig = 1.0 / (1.0 + jnp.exp(-pre))
@@ -230,7 +239,7 @@
 def grads_kernel(
     zt_ref, bc_ref, dyt_ref, der_ref, cl_ref, s_ref, a_ref, xw_ref, dw_ref,
     step_ref, rate_ref, skip_ref, xbc_ref, before_ref, w_ref,
-    gin_ref, edge_ref, front_ref, gstep_ref, gw_ref, grate_ref, gskip_ref,
+    gin_ref, edge_ref, front_ref, gstep_ref, pack_ref,
     gz_ref, wsum_ref, d_ref, q_ref, l_ref, k_ref,
 ):
     row = lax.broadcasted_iota(jnp.int32, (GROUP, GROUP), 0)
@@ -289,9 +298,21 @@
     glog = jnp.dot(d_ref[...], upper, precision=HI, preferred_element_type=F32)
     glog = glog + jnp.dot(q_ref[...], lower, precision=HI, preferred_element_type=F32)
     glog = glog + l_ref[...]
-    gstep_ref[...] = -rate_ref[...] * glog
-    grate_ref[...] = -jnp.sum(step_ref[...] * glog, axis=1, keepdims=True)
-    gskip_ref[...] = jnp.sum(k_ref[...], axis=1, keepdims=True)
+    d_ref[...] = glog
+
+    @pl.loop(0, HEADS)
+    def _(h):
+        one = pl.ds(h, 1)
+        gstep_ref[one, :] = -(d_ref[one, :] * rate_ref[h])
+
+    ones = jnp.ones((8, GROUP), F32)
+    sums = (-step_ref[...] * glog, k_ref[...])
+    for c in range(2):
+        line = lax.dot_general(
+            ones, sums[c], (((1,), (1,)), ((), ())), precision=HI, preferred_element_type=F32
+        )
+        line = jnp.concatenate([line[:1], jnp.zeros((1, STATE - HEADS), F32)], axis=1)
+        pack_ref[c, PACK - 1 : PACK, :] = line
 
     @pl.loop(0, CH // TILE)
     def _(i):
@@ -303,7 +324,7 @@
             off = KCONV - 1 - k
             gin = gin + w_ref[k : k + 1, cols] * padded[off : off + GROUP]
         gin_ref[:, cols] = gin.astype(BF16)
-        edge_ref[:, cols] = gin[GROUP - 8 :]
+        edge_ref[:, cols] = gin[GROUP - EDGE :]
         first = gp[:8]
         sub = lax.broadcasted_iota(jnp.int32, (8, TILE), 0)
         front_pad = jnp.concatenate([jnp.zeros((8, TILE), F32), first], axis=0)
@@ -314,9 +335,11 @@
             rim = rim + w_ref[k : k + 1, cols] * piece
         front_ref[:, cols] = rim
         x = jnp.concatenate([before_ref[:, cols].astype(F32), xbc_ref[:, cols].astype(F32)], axis=0)
-        for k in range(KCONV):
-            gw_ref[k : k + 1, cols] = jnp.sum(gp * x[5 + k : 5 + k + GROUP], axis=0, keepdims=True)
-        gw_ref[KCONV : KCONV + 1, cols] = jnp.sum(gp, axis=0, keepdims=True)
+        for k in range(KCONV + 1):
+            terms = gp * x[5 + k : 5 + k + GROUP] if k < KCONV else gp
+            line = jnp.sum(terms, axis=0, keepdims=True)
+            for c in range(2):
+                pack_ref[c, pl.ds(k * LINES + i, 1), :] = line[:, c * STATE : (c + 1) * STATE]
 
 
 def bits_of(n):
@@ -328,10 +351,11 @@
     return out
 
 
-def reduce_kernel(steps, pack_ref, front_ref, out_ref, rim_ref, acc, box, ssem, rsem, fs, fr):
+def reduce_kernel(steps, pack_ref, front_ref, out_ref, rim_ref, acc, box, ssem, rsem, fs, fr, gs, gr):
     pos = {"dp": lax.axis_index("dp"), "seq": lax.axis_index("seq")}
     n = lax.axis_size("seq")
     me = pos["seq"]
+    core = pos["dp"] % 2
     to = []
     for axis, b in steps:
         p = pos[axis]
@@ -363,18 +387,22 @@
     copies = []
     for i, where in enumerate(to):
         copy = pltpu.make_async_remote_copy(
-            src_ref=pack_ref if i == 0 else acc.at[i], dst_ref=box.at[i],
+            src_ref=pack_ref.at[1 - core] if i == 0 else acc.at[i], dst_ref=box.at[i],
             send_sem=ssem.at[i], recv_sem=rsem.at[i],
             device_id=where, device_id_type=MESH,
         )
         copy.start()
         copies.append(copy)
         copy.wait_recv()
-        total = (pack_ref[...] if i == 0 else acc[i]) + box[i]
-        if i + 1 < len(to):
-            acc[i + 1] = total
-        else:
-            out_ref[...] = total
+        total = (pack_ref[core] if i == 0 else acc[i]) + box[i]
+        acc[i + 1] = total
+    share = pltpu.make_async_remote_copy(
+        src_ref=acc.at[len(to)], dst_ref=out_ref.at[core], send_sem=gs, recv_sem=gr,
+        device_id=to[0], device_id_type=MESH,
+    )
+    share.start()
+    out_ref[core] = total
+    share.wait()
     for copy in copies:
         copy.wait_send()
 
@@ -389,6 +417,24 @@
     @pl.when(me == n - 1)
     def _():
         rim_ref[...] = jnp.zeros_like(rim_ref)
+
+
+def finish_kernel(
+    total_ref, edge_ref, rim_ref, gin_ref, out_ref, gw_ref, gb_ref, grate_ref, gskip_ref, last, sem
+):
+    final = edge_ref[...] + jnp.concatenate([jnp.zeros((8, CH), F32), rim_ref[...]], axis=0)
+    last[...] = final.astype(BF16)
+    copy = pltpu.make_async_copy(last, out_ref.at[pl.ds(GROUP - EDGE, EDGE)], sem)
+    copy.start()
+    for i in range(LINES):
+        for c in range(2):
+            cols = pl.ds((2 * i + c) * STATE, STATE)
+            for k in range(KCONV):
+                gw_ref[k : k + 1, cols] = total_ref[c, pl.ds(k * LINES + i, 1), :]
+            gb_ref[cols] = total_ref[c, KCONV * LINES + i, :]
+    grate_ref[...] = total_ref[0, PACK - 1, :HEADS]
+    gskip_ref[...] = total_ref[1, PACK - 1, :HEADS]
+    copy.wait()
 
 
 def sds(shape, dtype):
@@ -405,7 +451,6 @@
     xbc = xbc_in[0]
     dy = grad_out[0]
     step = step_sizes[0]
-    rate = decay_rates[:, None]
     state = (HEADS, HEAD_DIM, STATE)
     zt, bc, dyt, der, cl, s, u, decay, xw, dw = pl.pallas_call(
         locals_kernel,
@@ -415,10 +460,11 @@
             sds((XW, STATE), BF16), sds((HEADS, STATE), F32), sds((XW, GROUP), BF16),
             sds((XW, GROUP), BF16),
         ],
-        in_specs=[VM()] * 7,
+        in_specs=[VM()] * 5 + [SM(), VM()],
         out_specs=[VM()] * 10,
+        scratch_shapes=[pltpu.VMEM((HEADS, GROUP), F32)],
         compiler_params=pltpu.CompilerParams(vmem_limit_bytes=LIMIT),
-    )(xbc, before, conv_weight, conv_bias[None], step, rate, dy)
+    )(xbc, before, conv_weight, conv_bias, step, decay_rates, dy)
 
     half = (HALF, HEAD_DIM, STATE)
     dma = pltpu.SemaphoreType.DMA
@@ -437,43 +483,49 @@
         ),
     )(s.reshape(state), u.reshape(state), decay)
 
-    gin, edge, front, gstep, gw, grate, gskip = pl.pallas_call(
+    gin, edge, front, gstep, pack = pl.pallas_call(
         grads_kernel,
         out_shape=[
-            sds((GROUP, CH), BF16), sds((8, CH), F32), sds((8, CH), F32), sds((HEADS, GROUP), F32),
-            sds((KCONV + 1, CH), F32), sds((HEADS, 1), F32), sds((HEADS, 1), F32),
+            sds((GROUP, CH), BF16), sds((EDGE, CH), F32), sds((8, CH), F32), sds((HEADS, GROUP), F32),
+            sds((2, PACK, STATE), F32),
         ],
-        in_specs=[VM()] * 11 + [SM()] + [VM()] * 3,
-        out_specs=[VM()] * 7,
+        in_specs=[VM()] * 10 + [SM()] * 2 + [VM()] * 3,
+        out_specs=[VM()] * 5,
         scratch_shapes=[pltpu.VMEM((GROUP, CH), F32), pltpu.VMEM((GROUP, GROUP), F32)]
         + [pltpu.VMEM((HEADS, GROUP), F32)] * 4,
         compiler_params=pltpu.CompilerParams(vmem_limit_bytes=LIMIT),
     )(
         zt, bc, dyt, der, cl, start.reshape(XW, STATE), end.reshape(XW, STATE), xw, dw,
-        step, rate, skip_gain, xbc, before, conv_weight,
+        step, decay_rates, skip_gain, xbc, before, conv_weight,
     )
 
-    small = jnp.concatenate([grate[:, 0], gskip[:, 0], jnp.zeros((CH - 2 * HEADS,), F32)])
-    pack = jnp.concatenate([gw, small[None], jnp.zeros((2, CH), F32)], axis=0)
     steps = [("dp", b) for b in bits_of(lax.axis_size("dp"))]
     steps += [("seq", b) for b in bits_of(lax.axis_size("seq"))]
     count = len(steps)
     total, rim = pl.pallas_call(
         functools.partial(reduce_kernel, steps),
-        out_shape=[sds((8, CH), F32)] * 2,
+        out_shape=[sds((2, PACK, STATE), F32), sds((8, CH), F32)],
         in_specs=[VM()] * 2,
         out_specs=[VM()] * 2,
-        scratch_shapes=[pltpu.VMEM((count, 8, CH), F32)] * 2 + [dma((count,))] * 2 + [dma, dma],
+        scratch_shapes=[pltpu.VMEM((count + 1, PACK, STATE), F32)] * 2
+        + [dma((count,))] * 2
+        + [dma] * 4,
         compiler_params=pltpu.CompilerParams(
             vmem_limit_bytes=LIMIT, collective_id=1, has_side_effects=True
         ),
     )(pack, front)
-    final = (edge + rim).astype(BF16)
-    grad_in = lax.dynamic_update_slice(gin, final, (tokens - 8, 0))
-    return (
-        grad_in[None], gstep[None], total[:KCONV], total[KCONV],
-        total[KCONV + 1, :HEADS], total[KCONV + 1, HEADS : 2 * HEADS],
-    )
+    grad_in, gw, gb, grate, gskip = pl.pallas_call(
+        finish_kernel,
+        out_shape=[
+            sds((GROUP, CH), BF16), sds((KCONV, CH), F32), sds((CH,), F32),
+            sds((HEADS,), F32), sds((HEADS,), F32),
+        ],
+        in_specs=[VM()] * 3 + [pl.BlockSpec(memory_space=pl.ANY)],
+        out_specs=[pl.BlockSpec(memory_space=pl.ANY)] + [VM()] * 4,
+        scratch_shapes=[pltpu.VMEM((EDGE, CH), BF16), dma],
+        input_output_aliases={3: 0},
+    )(total, edge, rim, gin)
+    return (grad_in[None], gstep[None], gw, gb, grate, gskip)
 
 
 def solution(mesh):

time: 110 us -> 99 us (0.900)
  local copies, waits for them, and re-layouts: 8.61 us -> 1.41 us
  other arithmetic: 4.83 us -> 0 us
  waiting for transfers between devices: 0.01 us -> 1.69 us
    slice x2 -> x0, local copies, waits for them, and re-layouts: 3.04 us -> none  [the longest x1 1.52 us: shards(): total[KCONV]]
    broadcast_in_dim x5 -> x0, local copies, waits for them, and re-layouts: 2.67 us -> none  [the longest x1 1.34 us: shards(): rate = decay_rates[:, None]]
    ppermute x1, waiting for transfers between devices: 0.01 us -> 1.69 us  [shifted(): return lax.ppermute(array, axis, pairs)]
    pallas_call x2 -> x0, other arithmetic: 1.68 us -> none  [shards(): pl.pallas_call(grads_kernel, out_shape=[sds((GROUP, CH), BF16), sds((8, C...]
    concatenate x1 -> x0, other arithmetic: 1.59 us -> none  [shards(): pack = jnp.concatenate([gw, small[None], jnp.zeros((2, CH), F32)], axis=0)]
    dynamic_update_slice x1 -> x0, other arithmetic: 1.56 us -> none  [shards(): grad_in = lax.dynamic_update_slice(gin, final, (tokens - 8, 0))]
    squeeze x1 -> x0, local copies, waits for them, and re-layouts: 1.33 us -> none  [shards(): total[KCONV + 1, HEADS:2 * HEADS]]
    pallas_call x2 -> x3, Pallas kernels: 40.3 us -> 39.4 us  [the longest x1 19.6 us: shards(): pl.pallas_call(grads_kernel, out_shape=[sds((GROUP, CH), BF16), sds((EDGE...]
  transfers between devices with their start and end apart: 1 -> 1, of which waited for: 0 -> 1; matrix products, arithmetic and copies ran while one was open for 2% -> 0% of each run, Pallas kernels for 0% -> 0%
where the time goes in v2:
time: 99 us; the launch traced here: 98.6 us
  Pallas kernels  90 us (91%)
  starting transfers between devices  4.89 us (5%)
  waiting for transfers between devices  1.69 us (2%)
  local copies, waits for them, and re-layouts  1.41 us (1%)
    pallas_call x1, Pallas kernels, shards(): pl.pallas_call(states_kernel, out_shape=[sds(state, BF16)] * 2, in_specs=...  34.6 us
    pallas_call x1, Pallas kernels, shards(): pl.pallas_call(grads_kernel, out_shape=[sds((GROUP, CH), BF16), sds((EDGE...  19.6 us
    pallas_call x1, Pallas kernels, shards(): pl.pallas_call(functools.partial(reduce_kernel, steps), out_shape=[sds((2...  17.6 us
    pallas_call x1, Pallas kernels, shards(): pl.pallas_call(locals_kernel, out_shape=[sds((CH, GROUP), BF16), sds((GRO...  16 us
    ppermute x1, starting transfers between devices, shifted(): return lax.ppermute(array, axis, pairs)  4.89 us
    pallas_call x1, Pallas kernels, shards(): pl.pallas_call(finish_kernel, out_shape=[sds((GROUP, CH), BF16), sds((KCO...  2.3 us
  transfers between devices with their start and end apart: 1, of which 1 were waited for; matrix products, arithmetic and copies ran while one was open for 0% of the time, Pallas kernels for 0%

profile of v2, /device:TPU:0, one launch (start us, length us, event | category | flops | bytes accessed | tf_op | source)
XLA Modules:
  0.0 98.6 jit_solution(17652584284553234703)
XLA Ops:
  0.6 0.8 slice.3
  1.4 4.9 %collective-permute-start = (bf16[1,8,2816]{2,1,0:T(8,128)(2,1)S(1)}, bf16[1,8,2816]{2,1,0:T(8,128)(2,1)S(1)}, u32[]{:S(2)}, u32[]{:S(2)}) collective-permute-start(bf16[1,8,2816]{2,1,0:T(8,128)(2,1)S(1)} %slice.3), channel_id=1, source_target_pairs={{0,1},{1,2},{2,3},{3,4},{4,5},{5,6},{6,7},{8,9},{9,10},{10,11},{11... | collective-permute-start | bytes 135176 | tf_op jit(solution)/shard_map/ppermute | solution.py:38
  6.3 1.7 %collective-permute-done = bf16[1,8,2816]{2,1,0:T(8,128)(2,1)S(1)} collective-permute-done((bf16[1,8,2816]{2,1,0:T(8,128)(2,1)S(1)}, bf16[1,8,2816]{2,1,0:T(8,128)(2,1)S(1)}, u32[]{:S(2)}, u32[]{:S(2)}) %collective-permute-start) | collective-permute-done | bytes 45088 | tf_op jit(solution)/shard_map/ppermute | solution.py:38
  8.0 0.0 copy-start
  8.0 0.6 copy-done
  8.6 16.0 %shard_map.118 = (bf16[2816,256]{1,0:T(8,128)(2,1)}, bf16[256,256]{1,0:T(8,128)(2,1)}, bf16[2560,256]{1,0:T(8,128)(2,1)}, f32[256,2816]{1,0:T(8,128)}, f32[40,25...) custom-call(bf16[256,2816]{1,0:T(8,128)(2,1)} %bitcast.10, ...), custom_call_target="tpu_custom_call" | custom-call | tf_op jit(solution)/shard_map/pallas_call | solution.py:455
  24.6 34.6 %shard_map.119 = (bf16[40,64,128]{2,1,0:T(8,128)(2,1)}, bf16[40,64,128]{2,1,0:T(8,128)(2,1)}) custom-call(bf16[40,64,128]{2,1,0:T(8,128)(2,1)} %bitcast.16, bf16[40,64,128]{2,1,0:T(8,128)(2,1)} %bitcast.17, f32[40,128]{1,0:T(8,128)} %get-tuple-element.37.a_ref), custom_call_target="tpu_custom_call" | custom-call | tf_op jit(solution)/shard_map/pallas_call | solution.py:471
  59.2 19.6 %shard_map.120 = (bf16[256,2816]{1,0:T(8,128)(2,1)}, f32[16,2816]{1,0:T(8,128)}, f32[8,2816]{1,0:T(8,128)}, f32[40,256]{1,0:T(8,128)}, f32[2,56,128]{2,1,0:T(8,128)}) custom-call(bf16[2816,256]{1,0:T(8,128)(2,1)} %get-tuple-element.30.zt_ref, bf16[256,256]{1,0:T(8,128)(2,1)} %get-tuple-element.31.bc_ref, bf16[2560,256]{1,0:T(8,128)(2,1)} %get-tuple-element.32.dyt_ref, ...), custom_call_target="tpu_custom_call" | custom-call | tf_op jit(solution)/shard_map/pallas_call | solution.py:486
  78.8 17.6 %shard_map.121 = (f32[2,56,128]{2,1,0:T(8,128)}, f32[8,2816]{1,0:T(8,128)}) custom-call(f32[2,56,128]{2,1,0:T(8,128)} %get-tuple-element.42.pack_ref, f32[8,2816]{1,0:T(8,128)} %get-tuple-element.43.front_ref), custom_call_target="tpu_custom_call" | custom-call | tf_op jit(solution)/shard_map/pallas_call | solution.py:505
  96.3 2.3 %shard_map.122 = (bf16[256,2816]{1,0:T(8,128)(2,1)}, f32[4,2816]{1,0:T(4,128)}, f32[2816]{0:T(1024)}, f32[40]{0:T(128)}, f32[40]{0:T(128)}) custom-call(f32[2,56,128]{2,1,0:T(8,128)} %get-tuple-element.44.total_ref, f32[16,2816]{1,0:T(8,128)} %get-tuple-element.45.edge_ref, f32[8,2816]{1,0:T(8,128)} %get-tuple-element.46.rim_ref, ...), custom_call_target="tpu_custom_call", output_to_operand_aliasing={{0}: (3, {})} | custom-call | tf_op jit(solution)/shard_map/pallas_call | solution.py:517
Async XLA Ops:
  1.4 6.6 %collective-permute-start = (bf16[1,8,2816]{2,1,0:T(8,128)(2,1)S(1)}, bf16[1,8,2816]{2,1,0:T(8,128)(2,1)S(1)}, u32[]{:S(2)}, u32[]{:S(2)}) collective-permute-start(bf16[1,8,2816]{2,1,0:T(8,128)(2,1)S(1)} %slice.3), channel_id=1, source_target_pairs={{0,1},{1,2},{2,3},{3,4},{4,5},{5,6},{6,7},{8,9},{9,10},{10,11},{11... | collective-permute-start | bytes 135176 | tf_op jit(solution)/shard_map/ppermute | solution.py:38
  8.0 0.6 copy-start

commit v3 on v2

v3 whole, which is shorter than its diff:
```python
import functools
import jax
import jax.numpy as jnp
from jax import lax
from jax.experimental import pallas as pl
from jax.experimental.pallas import tpu as pltpu
from jax.sharding import PartitionSpec as P

HEADS = 40
HEAD_DIM = 64
STATE = 128
GROUP = 256
KCONV = 4
XW = HEADS * HEAD_DIM
CH = XW + 2 * STATE
TILE = 256
HALF = HEADS // 2
CHUNK = 5
EDGE = 16
LINES = CH // TILE
PACK = (KCONV + 1) * LINES + 1
NCHUNK = HALF // CHUNK
MESH = pl.DeviceIdType.MESH
F32 = jnp.float32
BF16 = jnp.bfloat16
HI = lax.Precision.HIGHEST
VM = functools.partial(pl.BlockSpec, memory_space=pltpu.VMEM)
SM = functools.partial(pl.BlockSpec, memory_space=pltpu.SMEM)


def dot(a, b, ca, cb):
    return lax.dot_general(a, b, (((ca,), (cb,)), ((), ())), preferred_element_type=F32)


def bits_of(n):
    out = []
    b = 1
    while b < n:
        out.append(b)
        b *= 2
    return out


def core_kernel(
    steps,
    xbc_ref, w_ref, bias_ref, step_ref, rate_ref, dy_ref, skip_ref,
    gin_ref, edge_ref, gstep_ref, out_ref, rim_ref,
    zt_ref, bc_ref, dyt_ref, der_ref, cl_ref, xw_ref, dw_ref, log_ref, before_ref,
    s_ref, u_ref, dec_ref, start_ref, end_ref,
    sp, up, ap, ein, gin, eout, gout, sout, uout,
    gram_ref, wsum_ref, intra_ref, gz_ref, d_ref, q_ref, l_ref, k_ref, front_ref, pack_ref,
    acc, box,
    send1, recv1, send2, recv2, send3, recv3, senda, recva,
    ssem, rsem, fs, fr, gs, gr, bs, br,
):
    pos = {"dp": lax.axis_index("dp"), "seq": lax.axis_index("seq")}
    me = pos["seq"]
    n = lax.axis_size("seq")
    core = pos["dp"] % 2
    y = me % 2
    z = me // 2
    nz = n // 2
    pair = me + 1 - 2 * y
    mine = y * HALF
    other = (1 - y) * HALF
    last = nz - 1
    low = z < nz - nz // 2
    to = []
    for axis, b in steps:
        p = pos[axis]
        to.append({axis: p + b * (1 - 2 * ((p // b) % 2))})
    barrier = pltpu.get_barrier_semaphore()
    for where in to + [{"seq": pair}]:
        pl.semaphore_signal(barrier, inc=1, device_id=where, device_id_type=MESH)
    edges = 0
    for by in (-2, -1, 1, 2):
        inside = me + by >= 0 if by < 0 else me + by < n
        edges = edges + jnp.where(inside, 1, 0)

        @pl.when(inside)
        def _():
            pl.semaphore_signal(barrier, inc=1, device_id={"seq": me + by}, device_id_type=MESH)

    pl.semaphore_wait(barrier, len(to) + 1 + edges)

    rim_in = pltpu.make_async_remote_copy(
        src_ref=xbc_ref.at[pl.ds(GROUP - 8, 8)], dst_ref=before_ref, send_sem=bs, recv_sem=br,
        device_id={"seq": me + 1}, device_id_type=MESH,
    )

    @pl.when(me < n - 1)
    def _():
        rim_in.start()

    row = lax.broadcasted_iota(jnp.int32, (GROUP, GROUP), 0)
    col = lax.broadcasted_iota(jnp.int32, (GROUP, GROUP), 1)
    causal = row >= col
    upper = (row <= col).astype(F32)

    @pl.loop(0, HEADS)
    def _(h):
        one = pl.ds(h, 1)
        log_ref[one, :] = -(step_ref[one, :] * rate_ref[h])

    cl_ref[...] = jnp.dot(log_ref[...], upper, precision=HI, preferred_element_type=F32)

    @pl.loop(0, XW // TILE)
    def _(i):
        cols = pl.ds(pl.multiple_of(i * TILE, TILE), TILE)
        dyt_ref[cols, :] = dy_ref[:, cols].astype(F32).T.astype(BF16)

    @pl.when(me == 0)
    def _():
        before_ref[...] = jnp.zeros_like(before_ref)

    @pl.when(me > 0)
    def _():
        rim_in.wait_recv()

    @pl.when(me < n - 1)
    def _():
        rim_in.wait_send()

    def send(src, dst, ss, rs, to):
        return pltpu.make_async_remote_copy(
            src_ref=src, dst_ref=dst, send_sem=ss, recv_sem=rs,
            device_id={"seq": to}, device_id_type=MESH,
        )

    def part(c):
        return pl.ds(c * CHUNK, CHUNK)

    def pair_copy(j, c):
        src, dst = ((s_ref, sp), (u_ref, up))[j]
        return send(
            src.at[pl.ds(other + c * CHUNK, CHUNK)], dst.at[part(c)],
            send1.at[j, c], recv1.at[j, c], pair,
        )

    def chain_copy(j, c):
        src, dst = ((eout, ein), (gout, gin))[j]
        return send(
            src.at[part(c)], dst.at[part(c)], send2.at[j, c], recv2.at[j, c],
            me + 2 if j == 0 else me - 2,
        )

    def back_copy(j, c):
        src, dst = ((sout, start_ref), (uout, end_ref))[j]
        return send(
            src.at[part(c)], dst.at[pl.ds(mine + c * CHUNK, CHUNK)],
            send3.at[j, c], recv3.at[j, c], pair,
        )

    decay_copy = send(dec_ref, ap, senda, recva, pair)

    def begin(j):
        @pl.loop(0, NCHUNK)
        def _(c):
            pair_copy(j, c).start()

    def run(j):
        has_in = z > 0 if j == 0 else z < last
        has_out = z < last if j == 0 else z > 0
        inbox, outbox = ((ein, eout), (gin, gout))[j]
        got, own, back, result = ((sp, s_ref, sout, start_ref), (up, u_ref, uout, end_ref))[j]

        @pl.when(jnp.logical_not(has_in))
        def _():
            inbox[...] = jnp.zeros_like(inbox)

        @pl.loop(0, NCHUNK)
        def _(c):
            pair_copy(j, c).wait_recv()
            here = pl.ds(mine + c * CHUNK, CHUNK)
            first = y == 0
            aa = dec_ref[here, :][:, None, :]
            bb = ap[here, :][:, None, :]
            a0 = jnp.where(first, aa, bb)
            a1 = jnp.where(first, bb, aa)
            vv = own[here].astype(F32)
            ww = got[part(c)].astype(F32)
            v0 = jnp.where(first, vv, ww)
            v1 = jnp.where(first, ww, vv)

            @pl.when(has_in)
            def _():
                chain_copy(j, c).wait_recv()

            carry = inbox[part(c)].astype(F32)
            if j == 0:
                near, far = carry, a0 * carry + v0
                leave = a1 * far + v1
                kept = jnp.where(first, near, far)
                given = jnp.where(first, far, near)
            else:
                far, near = carry, a1 * carry + v1
                leave = a0 * near + v0
                kept = jnp.where(first, near, far)
                given = jnp.where(first, far, near)
            outbox[part(c)] = leave.astype(BF16)

            @pl.when(has_out)
            def _():
                chain_copy(j, c).start()

            back[part(c)] = given.astype(BF16)
            back_copy(j, c).start()
            result[here] = kept.astype(BF16)

    def form(j):
        src, dst = ((xw_ref, s_ref), (dw_ref, u_ref))[j]
        cols = pl.ds(j * STATE, STATE)

        @pl.loop(0, XW // TILE)
        def _(i):
            rows = pl.ds(pl.multiple_of(i * TILE, TILE), TILE)
            value = dot(src[rows, :], bc_ref[:, cols], 1, 0).astype(BF16)
            dst[pl.ds(4 * i, 4)] = value.reshape(4, HEAD_DIM, STATE)

    def activate(cols):
        x = xbc_ref[:, cols].astype(F32)
        padded = jnp.concatenate([before_ref[:, cols].astype(F32), x], axis=0)
        pre = bias_ref[cols][None, :]
        for k in range(KCONV):
            pre = pre + w_ref[k : k + 1, cols] * padded[5 + k : 5 + k + GROUP]
        sig = 1.0 / (1.0 + jnp.exp(-pre))
        der_ref[:, cols] = sig * (1.0 + pre * (1.0 - sig))
        return pre * sig

    @pl.loop(0, XW // TILE)
    def _(i):
        cols = pl.ds(pl.multiple_of(i * TILE, TILE), TILE)
        zt_ref[cols, :] = activate(cols).T.astype(BF16)

    tail_z = activate(pl.ds(XW, TILE))
    bc_ref[...] = tail_z.astype(BF16)
    zt_ref[pl.ds(XW, TILE), :] = tail_z.T.astype(BF16)
    cum = cl_ref[...]
    dec_ref[...] = jnp.broadcast_to(jnp.exp(cum[:, GROUP - 1 : GROUP]), (HEADS, STATE))

    @pl.loop(0, HEADS)
    def _(h):
        rows = pl.ds(pl.multiple_of(h * HEAD_DIM, HEAD_DIM), HEAD_DIM)
        cl = cl_ref[pl.ds(h, 1), :]
        xw_ref[rows, :] = (
            zt_ref[rows, :].astype(F32) * jnp.exp(cl[:, GROUP - 1 : GROUP] - cl)
        ).astype(BF16)
        dw_ref[rows, :] = (dyt_ref[rows, :].astype(F32) * jnp.exp(cl)).astype(BF16)

    @pl.when(low)
    def _():
        form(0)
        begin(0)
        form(1)
        begin(1)

    @pl.when(jnp.logical_not(low))
    def _():
        form(1)
        begin(1)
        form(0)
        begin(0)

    decay_copy.start()
    bproj = bc_ref[:, :STATE]
    cproj = bc_ref[:, STATE:]
    gram_ref[...] = dot(cproj, bproj, 1, 1)
    wsum_ref[...] = jnp.zeros_like(wsum_ref)

    def inner_head(h):
        rows = pl.ds(pl.multiple_of(h * HEAD_DIM, HEAD_DIM), HEAD_DIM)
        xt = zt_ref[rows, :]
        dyt = dyt_ref[rows, :]
        cl = cl_ref[pl.ds(h, 1), :]
        wide = jnp.broadcast_to(cl, (STATE, GROUP)).T
        gap = jnp.concatenate([wide, wide], axis=1) - cl
        decay = jnp.where(causal, jnp.exp(gap), 0.0)
        kmat = (decay * gram_ref[...]).astype(BF16)
        intra = dot(dyt, kmat, 1, 0)
        yt = dot(xt, kmat, 1, 1)
        xf = xt.astype(F32)
        dyf = dyt.astype(F32)
        one = pl.ds(h, 1)
        intra_ref[rows, :] = intra
        d_ref[one, :] = jnp.sum(xf * intra - dyf * yt, axis=0, keepdims=True)
        k_ref[one, :] = jnp.sum(xf * dyf, axis=0, keepdims=True)
        return decay * dot(dyt, xt, 0, 0)

    def inner_heads(start):
        @pl.loop(0, HALF // 2)
        def _(i):
            h = start + 2 * i
            wsum_ref[...] += inner_head(h) + inner_head(h + 1)

    inner_heads(0)
    decay_copy.wait_recv()

    @pl.when(low)
    def _():
        run(0)

    @pl.when(jnp.logical_not(low))
    def _():
        run(1)

    inner_heads(HALF)

    @pl.when(low)
    def _():
        run(1)

    @pl.when(jnp.logical_not(low))
    def _():
        run(0)

    decay_copy.wait_send()
    for j in range(2):
        @pl.loop(0, NCHUNK)
        def _(c):
            pair_copy(j, c).wait_send()
            back_copy(j, c).wait()

            @pl.when(z < last if j == 0 else z > 0)
            def _():
                chain_copy(j, c).wait_send()


    def head(h):
        rows = pl.ds(pl.multiple_of(h * HEAD_DIM, HEAD_DIM), HEAD_DIM)
        cl = cl_ref[pl.ds(h, 1), :]
        adj = end_ref[h]
        sta = start_ref[h]
        badj = dot(adj, zt_ref[pl.ds(XW, STATE), :], 1, 0)
        cst = dot(sta, zt_ref[pl.ds(XW + STATE, STATE), :], 1, 0)
        log_end = cl[:, GROUP - 1 : GROUP]
        tail = jnp.exp(log_end - cl)
        xf = zt_ref[rows, :].astype(F32)
        dyf = dyt_ref[rows, :].astype(F32)
        rterm = tail * jnp.sum(xf * badj, axis=0, keepdims=True)
        qterm = jnp.exp(cl) * jnp.sum(dyf * cst, axis=0, keepdims=True)
        prod = adj.astype(F32) * sta.astype(F32)
        four = jnp.exp(log_end) * jnp.sum(jnp.sum(prod, axis=0, keepdims=True), axis=1, keepdims=True)
        one = pl.ds(h, 1)
        gain = d_ref[one, :] + rterm
        d_ref[one, :] = gain
        q_ref[one, :] = qterm
        l_ref[one, :] = four - gain
        return intra_ref[rows, :] + tail * badj + skip_ref[h] * dyf

    @pl.loop(0, HEADS // 2)
    def _(hp):
        both = jnp.concatenate([head(2 * hp), head(2 * hp + 1)], axis=0)
        gz_ref[:, pl.ds(pl.multiple_of(hp * STATE, STATE), STATE)] = both.T

    wlow = wsum_ref[...].astype(BF16)
    gb = dot(wlow, cproj, 0, 0) + dot(end_ref[...].reshape(XW, STATE), xw_ref[...], 0, 0).T
    gc = dot(wlow, bproj, 1, 0) + dot(start_ref[...].reshape(XW, STATE), dw_ref[...], 0, 0).T
    gz_ref[:, pl.ds(XW, STATE)] = gb
    gz_ref[:, pl.ds(XW + STATE, STATE)] = gc
    lower = (row >= col).astype(F32)
    glog = jnp.dot(d_ref[...], upper, precision=HI, preferred_element_type=F32)
    glog = glog + jnp.dot(q_ref[...], lower, precision=HI, preferred_element_type=F32)
    glog = glog + l_ref[...]
    d_ref[...] = glog

    @pl.loop(0, HEADS)
    def _(h):
        one = pl.ds(h, 1)
        gstep_ref[one, :] = -(d_ref[one, :] * rate_ref[h])

    ones = jnp.ones((8, GROUP), F32)
    sums = (-step_ref[...] * glog, k_ref[...])
    for c in range(2):
        line = lax.dot_general(
            ones, sums[c], (((1,), (1,)), ((), ())), precision=HI, preferred_element_type=F32
        )
        line = jnp.concatenate([line[:1], jnp.zeros((1, STATE - HEADS), F32)], axis=1)
        pack_ref[c, PACK - 1 : PACK, :] = line

    @pl.loop(0, CH // TILE)
    def _(i):
        cols = pl.ds(pl.multiple_of(i * TILE, TILE), TILE)
        gp = gz_ref[:, cols] * der_ref[:, cols]
        padded = jnp.concatenate([gp, jnp.zeros((8, TILE), F32)], axis=0)
        gin = w_ref[KCONV - 1 : KCONV, cols] * gp
        for k in range(KCONV - 1):
            off = KCONV - 1 - k
            gin = gin + w_ref[k : k + 1, cols] * padded[off : off + GROUP]
        gin_ref[:, cols] = gin.astype(BF16)
        edge_ref[:, cols] = gin[GROUP - EDGE :]
        first = gp[:8]
        sub = lax.broadcasted_iota(jnp.int32, (8, TILE), 0)
        front_pad = jnp.concatenate([jnp.zeros((8, TILE), F32), first], axis=0)
        rim = jnp.zeros((8, TILE), F32)
        for k in range(KCONV - 1):
            off = KCONV - 1 - k
            piece = jnp.where(sub >= 8 - off, front_pad[off : off + 8], 0.0)
            rim = rim + w_ref[k : k + 1, cols] * piece
        front_ref[:, cols] = rim
        x = jnp.concatenate([before_ref[:, cols].astype(F32), xbc_ref[:, cols].astype(F32)], axis=0)
        for k in range(KCONV + 1):
            terms = gp * x[5 + k : 5 + k + GROUP] if k < KCONV else gp
            line = jnp.sum(terms, axis=0, keepdims=True)
            for c in range(2):
                pack_ref[c, pl.ds(k * LINES + i, 1), :] = line[:, c * STATE : (c + 1) * STATE]

    rim = pltpu.make_async_remote_copy(
        src_ref=front_ref, dst_ref=rim_ref, send_sem=fs, recv_sem=fr,
        device_id={"seq": me - 1}, device_id_type=MESH,
    )

    @pl.when(me > 0)
    def _():
        rim.start()

    copies = []
    for i, where in enumerate(to):
        copy = pltpu.make_async_remote_copy(
            src_ref=pack_ref.at[1 - core] if i == 0 else acc.at[i], dst_ref=box.at[i],
            send_sem=ssem.at[i], recv_sem=rsem.at[i],
            device_id=where, device_id_type=MESH,
        )
        copy.start()
        copies.append(copy)
        copy.wait_recv()
        total = (pack_ref[core] if i == 0 else acc[i]) + box[i]
        acc[i + 1] = total
    share = pltpu.make_async_remote_copy(
        src_ref=acc.at[len(to)], dst_ref=out_ref.at[core], send_sem=gs, recv_sem=gr,
        device_id=to[0], device_id_type=MESH,
    )
    share.start()
    out_ref[core] = total
    share.wait()
    for copy in copies:
        copy.wait_send()

    @pl.when(me > 0)
    def _():
        rim.wait_send()

    @pl.when(me < n - 1)
    def _():
        rim.wait_recv()

    @pl.when(me == n - 1)
    def _():
        rim_ref[...] = jnp.zeros_like(rim_ref)


def finish_kernel(
    total_ref, edge_ref, rim_ref, gin_ref, out_ref, gw_ref, gb_ref, grate_ref, gskip_ref, last, sem
):
    final = edge_ref[...] + jnp.concatenate([jnp.zeros((8, CH), F32), rim_ref[...]], axis=0)
    last[...] = final.astype(BF16)
    copy = pltpu.make_async_copy(last, out_ref.at[pl.ds(GROUP - EDGE, EDGE)], sem)
    copy.start()
    for i in range(LINES):
        for c in range(2):
            cols = pl.ds((2 * i + c) * STATE, STATE)
            for k in range(KCONV):
                gw_ref[k : k + 1, cols] = total_ref[c, pl.ds(k * LINES + i, 1), :]
            gb_ref[cols] = total_ref[c, KCONV * LINES + i, :]
    grate_ref[...] = total_ref[0, PACK - 1, :HEADS]
    gskip_ref[...] = total_ref[1, PACK - 1, :HEADS]
    copy.wait()


def sds(shape, dtype):
    return jax.ShapeDtypeStruct(shape, dtype)


LIMIT = 62 * 1024 * 1024


def shards(xbc_in, conv_weight, conv_bias, step_sizes, decay_rates, skip_gain, grad_out):
    steps = [("dp", b) for b in bits_of(lax.axis_size("dp"))]
    steps += [("seq", b) for b in bits_of(lax.axis_size("seq"))]
    count = len(steps)
    state = (HEADS, HEAD_DIM, STATE)
    half = (HALF, HEAD_DIM, STATE)
    line = (HEADS, GROUP)
    dma = pltpu.SemaphoreType.DMA
    scratch = [
        ((CH, GROUP), BF16), ((GROUP, 2 * STATE), BF16), ((XW, GROUP), BF16), ((GROUP, CH), F32),
        (line, F32), ((XW, GROUP), BF16), ((XW, GROUP), BF16), (line, F32), ((8, CH), BF16),
        (state, BF16), (state, BF16), ((HEADS, STATE), F32), (state, BF16), (state, BF16),
        (half, BF16), (half, BF16), ((HEADS, STATE), F32),
    ]
    scratch += [(half, BF16)] * 6
    scratch += [((GROUP, GROUP), F32)] * 2 + [((XW, GROUP), F32), ((GROUP, CH), F32)]
    scratch += [(line, F32)] * 4 + [((8, CH), F32), ((2, PACK, STATE), F32)]
    scratch += [((count + 1, PACK, STATE), F32)] * 2
    gin, edge, gstep, total, rim = pl.pallas_call(
        functools.partial(core_kernel, steps),
        out_shape=[
            sds((GROUP, CH), BF16), sds((EDGE, CH), F32), sds((HEADS, GROUP), F32),
            sds((2, PACK, STATE), F32), sds((8, CH), F32),
        ],
        in_specs=[VM()] * 4 + [SM(), VM(), SM()],
        out_specs=[VM()] * 5,
        scratch_shapes=[pltpu.VMEM(*item) for item in scratch]
        + [dma((2, NCHUNK))] * 6
        + [dma] * 2
        + [dma((count,))] * 2
        + [dma] * 6,
        compiler_params=pltpu.CompilerParams(
            vmem_limit_bytes=LIMIT, collective_id=0, has_side_effects=True
        ),
    )(
        xbc_in[0], conv_weight, conv_bias, step_sizes[0], decay_rates, grad_out[0], skip_gain
    )
    grad_in, gw, gb, grate, gskip = pl.pallas_call(
        finish_kernel,
        out_shape=[
            sds((GROUP, CH), BF16), sds((KCONV, CH), F32), sds((CH,), F32),
            sds((HEADS,), F32), sds((HEADS,), F32),
        ],
        in_specs=[VM()] * 3 + [pl.BlockSpec(memory_space=pl.ANY)],
        out_specs=[pl.BlockSpec(memory_space=pl.ANY)] + [VM()] * 4,
        scratch_shapes=[pltpu.VMEM((EDGE, CH), BF16), dma],
        input_output_aliases={3: 0},
    )(total, edge, rim, gin)
    return (grad_in[None], gstep[None], gw, gb, grate, gskip)


def solution(mesh):
    return jax.shard_map(
        shards,
        mesh=mesh,
        in_specs=(
            P("dp", "seq", None), P(), P(), P("dp", None, "seq"), P(), P(), P("dp", "seq", None),
        ),
        out_specs=(P("dp", "seq", None), P("dp", None, "seq"), P(), P(), P(), P()),
        check_vma=False,
    )
```

time: 99 us -> 86.3 us (0.87)
  Pallas kernels: 90 us -> 82.3 us
  starting transfers between devices: 4.89 us -> 0 us
  local copies, waits for them, and re-layouts: 1.41 us -> 3.18 us
  waiting for transfers between devices: 1.69 us -> 0 us
    pallas_call x4 -> x1, Pallas kernels: 87.7 us -> 80 us  [shards(): pl.pallas_call(functools.partial(core_kernel, steps), out_shape=[sds((GRO...]
    ppermute x1 -> x0, starting transfers between devices: 4.89 us -> none  [shifted(): return lax.ppermute(array, axis, pairs)]
    unnamed x2 -> x4, local copies, waits for them, and re-layouts: 0.62 us -> 3.18 us
    ppermute x1 -> x0, waiting for transfers between devices: 1.69 us -> none  [shifted(): return lax.ppermute(array, axis, pairs)]
  transfers between devices with their start and end apart: 1 -> 0, of which waited for: 1 -> 0; matrix products, arithmetic and copies ran while one was open for 0% -> 0% of each run, Pallas kernels for 0% -> 0%
where the time goes in v3:
time: 86.3 us; the launch traced here: 86.1 us
  Pallas kernels  82.3 us (95%)
  local copies, waits for them, and re-layouts  3.18 us (4%)
    pallas_call x1, Pallas kernels, shards(): pl.pallas_call(functools.partial(core_kernel, steps), out_shape=[sds((GRO...  80 us
    unnamed x4, local copies, waits for them, and re-layouts  3.18 us
    pallas_call x1, Pallas kernels, shards(): pl.pallas_call(finish_kernel, out_shape=[sds((GROUP, CH), BF16), sds((KCO...  2.3 us

profile of v3, /device:TPU:0, one launch (start us, length us, event | category | flops | bytes accessed | tf_op | source)
XLA Modules:
  0.0 86.1 jit_solution(16257128080476887291)
XLA Ops:
  0.6 80.0 %shard_map.118 = (bf16[256,2816]{1,0:T(8,128)(2,1)}, f32[16,2816]{1,0:T(8,128)}, f32[40,256]{1,0:T(8,128)}, f32[2,56,128]{2,1,0:T(8,128)}, f32[8,2816]{1,0:T(8,128)}) custom-call(bf16[256,2816]{1,0:T(8,128)(2,1)} %bitcast.6, f32[4,2816]{1,0:T(4,128)} %w_ref.1, f32[2816]{0:T(1024)} %bias_ref.1, f32[40,256]{1,0:T(8,128)} %bitcast.9, f32[40]{0:T(128)} %rate_ref.1, ...), custom_call_target="tpu_custom_call" | custom-call | tf_op jit(solution)/shard_map/pallas_call | solution.py:494
  80.6 2.3 %shard_map.119 = (bf16[256,2816]{1,0:T(8,128)(2,1)}, f32[4,2816]{1,0:T(4,128)}, f32[2816]{0:T(1024)}, f32[40]{0:T(128)}, f32[40]{0:T(128)}) custom-call(f32[2,56,128]{2,1,0:T(8,128)} %get-tuple-element.16.total_ref, f32[16,2816]{1,0:T(8,128)} %get-tuple-element.17.edge_ref, f32[8,2816]{1,0:T(8,128)} %get-tuple-element.18.rim_ref, ...), custom_call_target="tpu_custom_call", output_to_operand_aliasing={{0}: (3, {})} | custom-call | tf_op jit(solution)/shard_map/pallas_call | solution.py:513
  82.9 0.0 copy-start
  82.9 2.6 %copy.17 = bf16[1,256,2816]{2,1,0:T(8,128)(2,1)} copy(bf16[1,256,2816]{2,1,0:T(8,128)(2,1)} %bitcast.5) | data formatting | bytes 2883584
  85.5 0.0 copy-done
  85.5 0.6 copy.18
Async XLA Ops:
  82.9 2.6 %copy-start = (f32[40,256]{1,0:T(8,128)S(1)}, f32[40,256]{1,0:T(8,128)}, u32[]{:S(2)}) copy-start(f32[40,256]{1,0:T(8,128)} %get-tuple-element.21) | copy-start | bytes 122884

commit v4 on v3

--- a/solution.py
+++ b/solution.py
@@ -15,7 +15,7 @@
 CH = XW + 2 * STATE
 TILE = 256
 HALF = HEADS // 2
-CHUNK = 5
+CHUNK = 2
 EDGE = 16
 LINES = CH // TILE
 PACK = (KCONV + 1) * LINES + 1
@@ -227,16 +227,25 @@
         der_ref[:, cols] = sig * (1.0 + pre * (1.0 - sig))
         return pre * sig
 
-    @pl.loop(0, XW // TILE)
-    def _(i):
-        cols = pl.ds(pl.multiple_of(i * TILE, TILE), TILE)
-        zt_ref[cols, :] = activate(cols).T.astype(BF16)
-
     tail_z = activate(pl.ds(XW, TILE))
     bc_ref[...] = tail_z.astype(BF16)
     zt_ref[pl.ds(XW, TILE), :] = tail_z.T.astype(BF16)
     cum = cl_ref[...]
     dec_ref[...] = jnp.broadcast_to(jnp.exp(cum[:, GROUP - 1 : GROUP]), (HEADS, STATE))
+
+    @pl.loop(0, HEADS)
+    def _(h):
+        rows = pl.ds(pl.multiple_of(h * HEAD_DIM, HEAD_DIM), HEAD_DIM)
+        cl = cl_ref[pl.ds(h, 1), :]
+        dw_ref[rows, :] = (dyt_ref[rows, :].astype(F32) * jnp.exp(cl)).astype(BF16)
+
+    form(1)
+    begin(1)
+
+    @pl.loop(0, XW // TILE)
+    def _(i):
+        cols = pl.ds(pl.multiple_of(i * TILE, TILE), TILE)
+        zt_ref[cols, :] = activate(cols).T.astype(BF16)
 
     @pl.loop(0, HEADS)
     def _(h):
@@ -245,21 +254,9 @@
         xw_ref[rows, :] = (
             zt_ref[rows, :].astype(F32) * jnp.exp(cl[:, GROUP - 1 : GROUP] - cl)
         ).astype(BF16)
-        dw_ref[rows, :] = (dyt_ref[rows, :].astype(F32) * jnp.exp(cl)).astype(BF16)
-
-    @pl.when(low)
-    def _():
-        form(0)
-        begin(0)
-        form(1)
-        begin(1)
-
-    @pl.when(jnp.logical_not(low))
-    def _():
-        form(1)
-        begin(1)
-        form(0)
-        begin(0)
+
+    form(0)
+    begin(0)
 
     decay_copy.start()
     bproj = bc_ref[:, :STATE]

time: 86.3 us -> 81.7 us (0.947)
  Pallas kernels: 82.3 us -> 77.7 us
    pallas_call x1, Pallas kernels: 80 us -> 75.3 us  [shards(): pl.pallas_call(functools.partial(core_kernel, steps), out_shape=[sds((GRO...]
where the time goes in v4:
time: 81.7 us; the launch traced here: 81.5 us
  Pallas kernels  77.7 us (95%)
  local copies, waits for them, and re-layouts  3.18 us (4%)
    pallas_call x1, Pallas kernels, shards(): pl.pallas_call(functools.partial(core_kernel, steps), out_shape=[sds((GRO...  75.3 us
    unnamed x4, local copies, waits for them, and re-layouts  3.18 us
    pallas_call x1, Pallas kernels, shards(): pl.pallas_call(finish_kernel, out_shape=[sds((GROUP, CH), BF16), sds((KCO...  2.3 us

profile of v4, /device:TPU:0, one launch (start us, length us, event | category | flops | bytes accessed | tf_op | source)
XLA Modules:
  0.0 81.5 jit_solution(528385652182079735)
XLA Ops:
  0.6 75.3 %shard_map.118 = (bf16[256,2816]{1,0:T(8,128)(2,1)}, f32[16,2816]{1,0:T(8,128)}, f32[40,256]{1,0:T(8,128)}, f32[2,56,128]{2,1,0:T(8,128)}, f32[8,2816]{1,0:T(8,128)}) custom-call(bf16[256,2816]{1,0:T(8,128)(2,1)} %bitcast.6, f32[4,2816]{1,0:T(4,128)} %w_ref.1, f32[2816]{0:T(1024)} %bias_ref.1, f32[40,256]{1,0:T(8,128)} %bitcast.9, f32[40]{0:T(128)} %rate_ref.1, ...), custom_call_target="tpu_custom_call" | custom-call | tf_op jit(solution)/shard_map/pallas_call | solution.py:491
  76.0 2.3 %shard_map.119 = (bf16[256,2816]{1,0:T(8,128)(2,1)}, f32[4,2816]{1,0:T(4,128)}, f32[2816]{0:T(1024)}, f32[40]{0:T(128)}, f32[40]{0:T(128)}) custom-call(f32[2,56,128]{2,1,0:T(8,128)} %get-tuple-element.16.total_ref, f32[16,2816]{1,0:T(8,128)} %get-tuple-element.17.edge_ref, f32[8,2816]{1,0:T(8,128)} %get-tuple-element.18.rim_ref, ...), custom_call_target="tpu_custom_call", output_to_operand_aliasing={{0}: (3, {})} | custom-call | tf_op jit(solution)/shard_map/pallas_call | solution.py:510
  78.3 0.0 copy-start
  78.3 2.6 %copy.17 = bf16[1,256,2816]{2,1,0:T(8,128)(2,1)} copy(bf16[1,256,2816]{2,1,0:T(8,128)(2,1)} %bitcast.5) | data formatting | bytes 2883584
  80.9 0.0 copy-done
  80.9 0.6 copy.18
Async XLA Ops:
  78.3 2.6 %copy-start = (f32[40,256]{1,0:T(8,128)S(1)}, f32[40,256]{1,0:T(8,128)}, u32[]{:S(2)}) copy-start(f32[40,256]{1,0:T(8,128)} %get-tuple-element.21) | copy-start | bytes 122884

commit v5 on v4

--- a/solution.py
+++ b/solution.py
@@ -284,10 +284,11 @@
         return decay * dot(dyt, xt, 0, 0)
 
     def inner_heads(start):
-        @pl.loop(0, HALF // 2)
+        @pl.loop(0, HALF // 4)
         def _(i):
-            h = start + 2 * i
-            wsum_ref[...] += inner_head(h) + inner_head(h + 1)
+            h = start + 4 * i
+            front = inner_head(h) + inner_head(h + 1)
+            wsum_ref[...] += front + (inner_head(h + 2) + inner_head(h + 3))
 
     inner_heads(0)
     decay_copy.wait_recv()
@@ -344,10 +345,10 @@
         l_ref[one, :] = four - gain
         return intra_ref[rows, :] + tail * badj + skip_ref[h] * dyf
 
-    @pl.loop(0, HEADS // 2)
+    @pl.loop(0, HEADS // 4)
     def _(hp):
-        both = jnp.concatenate([head(2 * hp), head(2 * hp + 1)], axis=0)
-        gz_ref[:, pl.ds(pl.multiple_of(hp * STATE, STATE), STATE)] = both.T
+        four = jnp.concatenate([head(4 * hp + j) for j in range(4)], axis=0)
+        gz_ref[:, pl.ds(pl.multiple_of(hp * TILE, TILE), TILE)] = four.T
 
     wlow = wsum_ref[...].astype(BF16)
     gb = dot(wlow, cproj, 0, 0) + dot(end_ref[...].reshape(XW, STATE), xw_ref[...], 0, 0).T

time: 81.7 us -> 78.9 us (0.966)
  Pallas kernels: 77.7 us -> 74.8 us
    pallas_call x1, Pallas kernels: 75.3 us -> 72.5 us  [shards(): pl.pallas_call(functools.partial(core_kernel, steps), out_shape=[sds((GRO...]
where the time goes in v5:
time: 78.9 us; the launch traced here: 78.7 us
  Pallas kernels  74.8 us (95%)
  local copies, waits for them, and re-layouts  3.18 us (4%)
    pallas_call x1, Pallas kernels, shards(): pl.pallas_call(functools.partial(core_kernel, steps), out_shape=[sds((GRO...  72.5 us
    unnamed x4, local copies, waits for them, and re-layouts  3.18 us
    pallas_call x1, Pallas kernels, shards(): pl.pallas_call(finish_kernel, out_shape=[sds((GROUP, CH), BF16), sds((KCO...  2.3 us

profile of v5, /device:TPU:0, one launch (start us, length us, event | category | flops | bytes accessed | tf_op | source)
XLA Modules:
  0.0 78.7 jit_solution(13587052149257477385)
XLA Ops:
  0.6 72.5 %shard_map.118 = (bf16[256,2816]{1,0:T(8,128)(2,1)}, f32[16,2816]{1,0:T(8,128)}, f32[40,256]{1,0:T(8,128)}, f32[2,56,128]{2,1,0:T(8,128)}, f32[8,2816]{1,0:T(8,128)}) custom-call(bf16[256,2816]{1,0:T(8,128)(2,1)} %bitcast.6, f32[4,2816]{1,0:T(4,128)} %w_ref.1, f32[2816]{0:T(1024)} %bias_ref.1, f32[40,256]{1,0:T(8,128)} %bitcast.9, f32[40]{0:T(128)} %rate_ref.1, ...), custom_call_target="tpu_custom_call" | custom-call | tf_op jit(solution)/shard_map/pallas_call | solution.py:492
  73.2 2.3 %shard_map.119 = (bf16[256,2816]{1,0:T(8,128)(2,1)}, f32[4,2816]{1,0:T(4,128)}, f32[2816]{0:T(1024)}, f32[40]{0:T(128)}, f32[40]{0:T(128)}) custom-call(f32[2,56,128]{2,1,0:T(8,128)} %get-tuple-element.16.total_ref, f32[16,2816]{1,0:T(8,128)} %get-tuple-element.17.edge_ref, f32[8,2816]{1,0:T(8,128)} %get-tuple-element.18.rim_ref, ...), custom_call_target="tpu_custom_call", output_to_operand_aliasing={{0}: (3, {})} | custom-call | tf_op jit(solution)/shard_map/pallas_call | solution.py:511
  75.5 0.0 copy-start
  75.5 2.6 %copy.17 = bf16[1,256,2816]{2,1,0:T(8,128)(2,1)} copy(bf16[1,256,2816]{2,1,0:T(8,128)(2,1)} %bitcast.5) | data formatting | bytes 2883584
  78.1 0.0 copy-done
  78.1 0.6 copy.18
Async XLA Ops:
  75.5 2.6 %copy-start = (f32[40,256]{1,0:T(8,128)S(1)}, f32[40,256]{1,0:T(8,128)}, u32[]{:S(2)}) copy-start(f32[40,256]{1,0:T(8,128)} %get-tuple-element.21) | copy-start | bytes 122884
